TPU v7x, 512 devices: a whole 4x4x16 slice. The times are simulated.
512 devices in a mesh: seq: 64 (over z, y), ch: 8 (over x, core).
Axes of the slice: x: 4, y: 4, z: 16, core: 2. Of those that a mesh axis runs over, the one named last changes fastest.
Arguments:
- q_proj: bfloat16 [8192, 4096], P('seq', 'ch'), may hold values from -16 to 16
- k_proj: bfloat16 [8192, 4096], P('seq', 'ch'), may hold values from -6 to 6
- v_proj: bfloat16 [8192, 4096], P('seq', 'ch'), may hold values from -6 to 6
- feat_filter: float32 [3, 3, 4096], P(None, None, 'ch'), may hold values from -3.5 to 3.5
- long_filter: float32 [8192, 4096], P('seq', 'ch'), may hold values from -0.0625 to 0.0625
- skip_bias: float32 [4096], P('ch'), may hold values from -4 to 4
- norm_gain: float32 [4096], P('ch'), may hold values from 0.1 to 1.9
Outputs:
- mixed_out: bfloat16 [8192, 4096], P('seq', 'ch')
- normed: bfloat16 [8192, 4096], P('seq', 'ch')
All inputs are finite; a program needn't handle non-finite values.
Results may differ from a plain program's by a relative error of at most 0.015.
Values may be sent and summed in bfloat16 or wider, within the bound.
No kernel may reach another device: no remote copies, remote signals or barrier semaphores. Data moves between devices by JAX's collectives and lax.ppermute only.
A program may use at most 64 MiB of HBM per device.

v0:
```python
import math

import jax
import jax.numpy as jnp
from jax import lax
from jax.sharding import PartitionSpec as P

D = 4096


highest_precision = lax.Precision.HIGHEST


def shifted(block, axis, distance):
    devices = range(lax.axis_size(axis))
    route = [(i - distance, i) for i in devices if i - distance in devices]
    return lax.ppermute(block, axis, route)


def for_sending(value):
    return jax.tree.map(lambda a: a.astype(jnp.bfloat16) if a.dtype == jnp.float32 else a, value)


def angle_table(count, left, right):
    product = left[:, None] * right[None, :] % count
    angle = product.astype(jnp.float32) * (2.0 * math.pi / count)
    return (jnp.cos(angle), jnp.sin(angle))


def contract(pattern, table, values):
    return jnp.einsum(pattern, table, values, precision=highest_precision)


def rotate(pattern, cos_table, sin_table, real_part, imag_part, turning):
    out_real = contract(pattern, cos_table, real_part) - turning * contract(
        pattern, sin_table, imag_part
    )
    out_imag = contract(pattern, cos_table, imag_part) + turning * contract(
        pattern, sin_table, real_part
    )
    return (out_real, out_imag)


def frequency_order(groups):
    return jnp.arange(2 * groups, dtype=jnp.int32)


def shards(q_proj, k_proj, v_proj, feat_filter, long_filter, skip_bias, norm_gain):
    rows = q_proj.shape[0]
    taps = feat_filter.shape[1]
    groups = lax.axis_size("seq")
    stacked = jnp.stack([q_proj, k_proj, v_proj])
    previous = shifted(stacked[:, rows - (taps - 1) :, :], "seq", 1)
    extended = jnp.concatenate([previous, stacked], axis=1)
    featured = jnp.zeros(stacked.shape, jnp.float32)
    for offset in range(taps):
        window = extended[:, taps - 1 - offset : taps - 1 - offset + rows, :]
        featured = featured + feat_filter[:, offset, None, :] * window.astype(jnp.float32)
    query = featured[0]
    gated = featured[1] * featured[2]
    device = lax.axis_index("seq")
    per_device = rows // groups
    length = 2 * rows * groups
    order = frequency_order(groups)
    blocks = jnp.arange(groups, dtype=jnp.int32)
    within = jnp.arange(rows, dtype=jnp.int32)
    local_rows = device * per_device + jnp.arange(per_device, dtype=jnp.int32)
    slots = lax.dynamic_slice_in_dim(order, 2 * device, 2)
    cos_a, sin_a = angle_table(2 * groups, order, blocks)
    cos_w, sin_w = angle_table(length, order, local_rows)
    cos_b, sin_b = angle_table(rows, within, within)
    cos_v, sin_v = angle_table(length, slots, within)
    cos_i, sin_i = angle_table(2 * groups, blocks, order)
    signals = jnp.stack([gated, long_filter])[:, None]
    pieces = lax.all_to_all(
        signals.astype(jnp.bfloat16), "seq", split_axis=2, concat_axis=1, tiled=True
    ).astype(signals.dtype)
    real_part = contract("ka,xabc->xkbc", cos_a, pieces)
    imag_part = -contract("ka,xabc->xkbc", sin_a, pieces)
    cosine = cos_w[:, :, None]
    sine = sin_w[:, :, None]
    real_part, imag_part = (
        real_part * cosine + imag_part * sine,
        imag_part * cosine - real_part * sine,
    )
    spread = jnp.stack([real_part, imag_part], axis=1)
    pieces = lax.all_to_all(
        for_sending(spread), "seq", split_axis=2, concat_axis=3, tiled=True
    ).astype(spread.dtype)
    real_part, imag_part = rotate("kb,xsbc->xskc", cos_b, sin_b, pieces[:, 0], pieces[:, 1], -1.0)
    prod_real = real_part[0] * real_part[1] - imag_part[0] * imag_part[1]
    prod_imag = real_part[0] * imag_part[1] + imag_part[0] * real_part[1]
    real_part = prod_real
    imag_part = prod_imag
    real_part, imag_part = rotate("bk,skc->sbc", cos_b, sin_b, real_part, imag_part, 1.0)
    cosine = cos_v[:, :, None]
    sine = sin_v[:, :, None]
    spectra = jnp.stack(
        [real_part * cosine - imag_part * sine, imag_part * cosine + real_part * sine]
    )
    pieces = lax.all_to_all(
        for_sending(spectra), "seq", split_axis=2, concat_axis=1, tiled=True
    ).astype(spectra.dtype)
    summed = contract("ak,kbc->abc", cos_i, pieces[0]) - contract("ak,kbc->abc", sin_i, pieces[1])
    returned = summed / length
    long_conv = lax.all_to_all(
        for_sending(returned), "seq", split_axis=0, concat_axis=1, tiled=True
    ).astype(returned.dtype)[0]
    mixed = query * (long_conv + skip_bias * gated)
    squares = lax.psum(jnp.sum(mixed * mixed, axis=1), "ch")
    scale = lax.rsqrt(squares / D + 1e-05)
    normed = (mixed * scale[:, None] * norm_gain).astype(jnp.bfloat16)
    return (mixed.astype(jnp.bfloat16), normed)


def solution(mesh):
    return jax.shard_map(
        shards,
        mesh=mesh,
        in_specs=(
            P("seq", "ch"),
            P("seq", "ch"),
            P("seq", "ch"),
            P(None, None, "ch"),
            P("seq", "ch"),
            P("ch"),
            P("ch"),
        ),
        out_specs=(P("seq", "ch"), P("seq", "ch")),
        check_vma=False,
    )
```

profile of v0, /device:TPU:1, one launch (start us, length us, event | category | flops | bytes accessed | tf_op | source)
XLA Modules:
  0.0 198.7 jit_solution(11288892288786219012)
XLA Ops:
  0.6 0.0 copy-start.4
  0.6 0.0 copy-start.3
  0.6 1.1 pad_maximum_fusion.2
  1.8 4.0 %collective-permute-start = (bf16[3,2,512]{2,1,0:T(2,128)(2,1)S(1)}, bf16[3,2,512]{2,1,0:T(2,128)(2,1)S(1)}, u32[]{:S(2)}, u32[]{:S(2)}) collective-permute-start(bf16[3,2,512]{2,1,0:T(2,128)(2,1)S(1)} %slice.74), channel_id=1, source_target_pairs={{0,8},{8,16},{16,24},{24,32},{32,40},{40,48},{48,56},{56,64},{64,7... | collective-permute-start | bytes 18440 | tf_op jit(solution)/shard_map/ppermute | solution.py:17
  5.8 0.0 copy-done.4
  5.9 0.0 copy-done.3
  5.9 0.0 copy-start
  5.9 0.0 copy-start.1
  5.9 0.0 copy-start.2
  6.0 0.6 collective-permute-done
  6.6 0.2 copy-done
  6.8 0.1 copy-done.1
  6.8 0.1 copy-done.2
  6.9 0.1 maximum_maximum_fusion
  7.0 0.2 multiply_add_fusion
  7.3 1.0 copy.36
  8.3 19.2 %all-to-all-start = ((bf16[2,1,128,512]{3,0,1,2:T(2,128)(2,1)}), bf16[2,1,128,512]{3,0,1,2:T(2,128)(2,1)S(1)}, u32[]{:S(2)}, u32[]{:S(2)}) async-start(bf16[2,1,128,512]{3,0,1,2:T(2,128)(2,1)} %copy.36), calls=%async_computation | async-start | bytes 524288 | tf_op jit(solution)/shard_map/all_to_all | solution.py:75
  27.6 0.1 fusion.85
  27.7 18.1 %all-to-all-done = bf16[2,1,128,512]{3,0,1,2:T(2,128)(2,1)S(1)} async-done(((bf16[2,1,128,512]{3,0,1,2:T(2,128)(2,1)}), bf16[2,1,128,512]{3,0,1,2:T(2,128)(2,1)S(1)}, u32[]{:S(2)}, u32[]{:S(2)}) %all-to-all-start) | async-done | bytes 262176 | tf_op jit(solution)/shard_map/all_to_all | solution.py:75
  45.8 0.7 fusion
  46.5 0.9 fusion.7
  47.5 0.1 pad_maximum_fusion
  47.6 2.1 %copy.39 = bf16[2,2,128,2,512]{4,3,0,1,2:T(2,128)(2,1)} copy(bf16[2,2,128,2,512]{2,4,3,0,1:T(8,128)(2,1)S(1)} %pad_maximum_fusion) | data formatting | bytes 2097152 | tf_op jit(solution)/shard_map/stack | solution.py:86
  49.6 7.8 %all-to-all-start.1 = ((bf16[2,2,128,2,512]{4,3,0,1,2:T(2,128)(2,1)}), bf16[2,2,128,2,512]{4,3,0,1,2:T(2,128)(2,1)S(1)}, u32[]{:S(2)}, u32[]{:S(2)}) async-start(bf16[2,2,128,2,512]{4,3,0,1,2:T(2,128)(2,1)} %copy.39), calls=%async_computation.1 | async-start | bytes 2097152 | tf_op jit(solution)/shard_map/all_to_all | solution.py:87
  57.4 0.1 dynamic_slice.3
  57.5 0.1 fusion.83
  57.6 50.2 %all-to-all-done.1 = bf16[2,2,128,2,512]{4,3,0,1,2:T(2,128)(2,1)S(1)} async-done(((bf16[2,2,128,2,512]{4,3,0,1,2:T(2,128)(2,1)}), bf16[2,2,128,2,512]{4,3,0,1,2:T(2,128)(2,1)S(1)}, u32[]{:S(2)}, u32[]{:S(2)}) %all-to-all-start.1) | async-done | bytes 1048608 | tf_op jit(solution)/shard_map/all_to_all | solution.py:87
  107.9 1.1 copy.41
  108.9 0.7 fusion.135
  109.7 0.5 copy.57
  110.2 0.8 fusion.19
  111.0 0.5 copy.58
  111.5 0.8 fusion.15
  112.3 0.8 fusion.4
  113.2 0.8 fusion.2
  114.0 0.1 multiply_add_fusion.1
  114.2 0.8 fusion.9
  115.0 0.8 fusion.13
  115.8 0.8 convolution_add_fusion
  116.6 0.9 fusion.21
  117.5 0.1 pad_maximum_fusion.1
  117.6 0.5 copy.44
  118.1 36.8 %all_to_all.54 = bf16[2,2,128,512]{3,1,0,2:T(2,128)(2,1)S(1)} all-to-all(bf16[2,2,128,512]{3,1,0,2:T(2,128)(2,1)S(1)} %copy.44), channel_id=1, replica_groups=mesh['seq'=64,'ch'=8] {'seq'}, dimensions={2} | all-to-all | bytes 1048576 | tf_op jit(solution)/shard_map/all_to_all | solution.py:101
  154.9 0.4 copy.45
  155.3 0.4 fusion.136
  155.7 0.2 copy.46
  155.8 0.1 squeeze.13
  156.0 0.4 fusion.50
  156.3 0.2 copy.47
  156.5 0.1 squeeze.14
  156.6 0.4 fusion.6
  157.0 0.1 copy.48
  157.2 23.5 %all_to_all.55 = bf16[64,2,512]{2,1,0:T(2,128)(2,1)S(1)} all-to-all(bf16[64,2,512]{2,1,0:T(2,128)(2,1)S(1)} %copy.48), channel_id=1, replica_groups=mesh['seq'=64,'ch'=8] {'seq'}, dimensions={0} | all-to-all | bytes 262144 | tf_op jit(solution)/shard_map/all_to_all | solution.py:106
  180.7 0.0 copy-start.5
  180.8 0.6 copy-done.5
  181.4 0.1 multiply_reduce_fusion
  181.5 15.8 %psum.7 = f32[128]{0:T(128)S(1)} all-reduce(f32[128]{0:T(128)S(1)} %get-tuple-element.2), channel_id=1, replica_groups=mesh['seq'=64,'ch'=8] {'ch'}, use_global_device_ids=true, to_apply=%region_1.2 | all-reduce | flops 128 | bytes 1024 | tf_op jit(solution)/shard_map/psum | solution.py:110
  197.3 0.0 copy-start.6
  197.3 0.7 copy-done.6
  198.0 0.7 multiply_convert_fusion
  (11 shorter events, 0.2 us)
Async XLA Ops:
  0.6 5.2 %copy-start.4 = (f32[3,3,512]{2,1,0:T(4,128)S(1)}, f32[3,3,512]{2,1,0:T(4,128)}, u32[]{:S(2)}) copy-start(f32[3,3,512]{2,1,0:T(4,128)} %param.10) | copy-start | bytes 55300
  0.6 5.2 %copy-start.3 = (f32[128,512]{1,0:T(8,128)S(1)}, f32[128,512]{1,0:T(8,128)}, u32[]{:S(2)}) copy-start(f32[128,512]{1,0:T(8,128)} %param.11) | copy-start | bytes 786436
  1.8 4.8 %collective-permute-start = (bf16[3,2,512]{2,1,0:T(2,128)(2,1)S(1)}, bf16[3,2,512]{2,1,0:T(2,128)(2,1)S(1)}, u32[]{:S(2)}, u32[]{:S(2)}) collective-permute-start(bf16[3,2,512]{2,1,0:T(2,128)(2,1)S(1)} %slice.74), channel_id=1, source_target_pairs={{0,8},{8,16},{16,24},{24,32},{32,40},{40,48},{48,56},{56,64},{64,7... | collective-permute-start | bytes 18440 | tf_op jit(solution)/shard_map/ppermute | solution.py:17
  5.9 0.9 copy-start
  5.9 1.0 copy-start.1
  5.9 1.0 copy-start.2
  8.3 37.5 %all-to-all-start = ((bf16[2,1,128,512]{3,0,1,2:T(2,128)(2,1)}), bf16[2,1,128,512]{3,0,1,2:T(2,128)(2,1)S(1)}, u32[]{:S(2)}, u32[]{:S(2)}) async-start(bf16[2,1,128,512]{3,0,1,2:T(2,128)(2,1)} %copy.36), calls=%async_computation | async-start | bytes 524288 | tf_op jit(solution)/shard_map/all_to_all | solution.py:75
  49.6 58.2 %all-to-all-start.1 = ((bf16[2,2,128,2,512]{4,3,0,1,2:T(2,128)(2,1)}), bf16[2,2,128,2,512]{4,3,0,1,2:T(2,128)(2,1)S(1)}, u32[]{:S(2)}, u32[]{:S(2)}) async-start(bf16[2,2,128,2,512]{4,3,0,1,2:T(2,128)(2,1)} %copy.39), calls=%async_computation.1 | async-start | bytes 2097152 | tf_op jit(solution)/shard_map/all_to_all | solution.py:87
  180.7 0.7 copy-start.5
  197.3 0.7 copy-start.6
where the time goes:
time: 199 us
  blocking collectives  76.1 us (38%)
  waiting for transfers between devices  68.9 us (35%)
  starting transfers between devices  31.1 us (16%)
  local copies, waits for them, and re-layouts  9.55 us (5%)
  matrix products  9.14 us (5%)
  other arithmetic  2.94 us (1%)
    all_to_all x1, waiting for transfers between devices, shards(): lax.all_to_all(for_sending(spread), 'seq', split_axis=2, concat_axis=3, t...  50.2 us
    all_to_all x1, blocking collectives, shards(): lax.all_to_all(for_sending(spectra), 'seq', split_axis=2, concat_axis=1,...  36.8 us
    all_to_all x1, blocking collectives, shards(): lax.all_to_all(for_sending(returned), 'seq', split_axis=0, concat_axis=1,...  23.5 us
    all_to_all x1, starting transfers between devices, shards(): lax.all_to_all(signals.astype(jnp.bfloat16), 'seq', split_axis=2, concat_...  19.2 us
    all_to_all x1, waiting for transfers between devices, shards(): lax.all_to_all(signals.astype(jnp.bfloat16), 'seq', split_axis=2, concat_...  18.1 us
    psum x1, blocking collectives, shards(): squares = lax.psum(jnp.sum(mixed * mixed, axis=1), 'ch')  15.8 us
    dot_general x12, matrix products, contract(): return jnp.einsum(pattern, table, values, precision=highest_precision)  9.14 us
    all_to_all x1, starting transfers between devices, shards(): lax.all_to_all(for_sending(spread), 'seq', split_axis=2, concat_axis=3, t...  7.81 us
  transfers between devices with their start and end apart: 3, of which 3 were waited for; matrix products, arithmetic and copies ran while one was open for 0% of the time, Pallas kernels for 0%

commit v1 on v0

v1 whole, which is shorter than its diff:
```python
import jax
import jax.numpy as jnp
from jax import lax
from jax.experimental import pallas as pl
from jax.experimental.pallas import tpu as pltpu
from jax.sharding import PartitionSpec as P

EPS = 1e-05
F32 = jnp.float32
BF16 = jnp.bfloat16
VMEM = pl.BlockSpec(memory_space=pltpu.VMEM)


def shift_down(block, count):
    return jnp.concatenate([jnp.zeros((count, block.shape[1]), block.dtype), block[:-count]], axis=0)


def featured(stream_ref, halo, taps_ref, stream, padded):
    rows = stream_ref.shape[0]
    block = stream_ref[...].astype(F32)
    padded[8:, :] = block
    padded[6:8, :] = halo.astype(F32)
    out = taps_ref[stream, 0:1, :] * block
    out = out + taps_ref[stream, 1:2, :] * padded[7 : 7 + rows, :]
    return out + taps_ref[stream, 2:3, :] * padded[6 : 6 + rows, :]


def before_kernel(k_ref, v_ref, halo_ref, taps_ref, filter_ref, sent_ref, gated_ref, padded):
    rows, channels = k_ref.shape
    groups = sent_ref.shape[0]
    key = featured(k_ref, halo_ref[2:4, :], taps_ref, 1, padded)
    value = featured(v_ref, halo_ref[4:6, :], taps_ref, 2, padded)
    gated = key * value
    gated_ref[...] = gated
    down = lax.broadcasted_iota(jnp.int32, (rows, rows), 0)
    across = lax.broadcasted_iota(jnp.int32, (rows, rows), 1)
    backwards = (down + across == rows - 1).astype(BF16)
    taps = jnp.dot(backwards, filter_ref[...].astype(BF16), preferred_element_type=F32)
    signal = gated.T.reshape(groups, channels // groups, rows)
    taps = taps.T.reshape(groups, channels // groups, rows)
    sent_ref[...] = jnp.concatenate([signal, taps], axis=1).astype(BF16)


def conv_kernel(got_ref, out_ref, signal, taps, result):
    blocks, both, size = got_ref.shape
    each = both // 2
    half = size // 2
    got = got_ref[...].astype(F32)
    signal[...] = got[:, :each, :].reshape(blocks * each, size)
    taps[...] = got[:, each:, :].reshape(blocks * each, size)
    row = lax.broadcasted_iota(jnp.int32, (half, size), 0)
    lane = lax.broadcasted_iota(jnp.int32, (half, size), 1)
    own = lane < row + half + 1
    low = lane < half
    column = lane % half

    def channel(c, carry):
        now = signal[pl.ds(c, blocks, stride=each), :]
        once = shift_down(now, 1)
        twice = shift_down(now, 2)
        now_r, once_r, twice_r = (pltpu.roll(a, half, 1) for a in (now, once, twice))
        first = jnp.concatenate([jnp.where(low, twice_r, once_r), jnp.where(low, once_r, now_r)], axis=1)
        second = jnp.concatenate([once, now], axis=1)
        windows = jnp.concatenate([first, second], axis=0).astype(BF16)
        total = jnp.zeros((half, size), F32)
        before = jnp.zeros((half, size), F32)
        below = None
        for d in range(blocks):
            spread = jnp.broadcast_to(taps[pl.ds(each * d + c, 1), :], (half, size))
            turned = pltpu.roll(spread, half + 1, 1, stride=1, stride_axis=0)
            toeplitz = jnp.where(own, turned, before).astype(BF16)
            before = turned
            if d % 2 == 0:
                below = toeplitz
                continue
            product = lax.dot_general(
                jnp.concatenate([toeplitz, below], axis=1),
                windows,
                (((1,), (1,)), ((), ())),
                preferred_element_type=F32,
            )
            if d > 1:
                product = jnp.where(column >= d - 1, pltpu.roll(product, d - 1, 1), 0.0)
            total = total + product
        turned_back = total.T
        result[pl.ds(c, blocks, stride=each), :] = jnp.concatenate(
            [turned_back[:blocks], turned_back[blocks:]], axis=1
        )
        return carry

    lax.fori_loop(0, each, channel, 0)
    out_ref[...] = result[...].reshape(blocks, each, size).astype(BF16)


def mix_kernel(back_ref, q_ref, halo_ref, taps_ref, gated_ref, bias_ref, mixed_ref, rounded_ref, squares_ref, padded):
    rows, channels = q_ref.shape
    query = featured(q_ref, halo_ref[0:2, :], taps_ref, 0, padded)
    long_conv = back_ref[...].astype(F32).reshape(channels, rows).T
    mixed = query * (long_conv + bias_ref[...] * gated_ref[...])
    mixed_ref[...] = mixed
    rounded_ref[...] = mixed.astype(BF16)
    sums = jnp.sum(mixed * mixed, axis=1, keepdims=True)
    squares_ref[...] = jnp.broadcast_to(sums, (rows, rows)).T[0:1, :]


def norm_kernel(total, squares_ref, mixed_ref, gain_ref, out_ref):
    rows = mixed_ref.shape[0]
    squares = jnp.sum(squares_ref[...], axis=0)
    scale = lax.rsqrt(squares / total + EPS)
    scale = jnp.broadcast_to(scale, (rows, rows)).T[:, 0:1]
    out_ref[...] = (mixed_ref[...] * scale * gain_ref[...]).astype(BF16)


def shards(q_proj, k_proj, v_proj, feat_filter, long_filter, skip_bias, norm_gain):
    rows, channels = q_proj.shape
    taps = feat_filter.shape[1]
    groups = lax.axis_size("seq")
    columns = lax.axis_size("ch")
    each = channels // groups
    tail = jnp.concatenate([a[rows - (taps - 1) :, :] for a in (q_proj, k_proj, v_proj)], axis=0)
    halo = lax.ppermute(tail, "seq", [(i, i + 1) for i in range(groups - 1)])
    padded = pltpu.VMEM((rows + 8, channels), F32)
    sent, gated = pl.pallas_call(
        before_kernel,
        out_shape=(
            jax.ShapeDtypeStruct((groups, 2 * each, rows), BF16),
            jax.ShapeDtypeStruct((rows, channels), F32),
        ),
        in_specs=[VMEM] * 5,
        out_specs=(VMEM, VMEM),
        scratch_shapes=[padded],
        name="before",
    )(k_proj, v_proj, halo, feat_filter, long_filter)
    got = lax.all_to_all(sent, "seq", split_axis=0, concat_axis=0, tiled=True)
    scratch = pltpu.VMEM((groups * each, rows), F32)
    conv = pl.pallas_call(
        conv_kernel,
        out_shape=jax.ShapeDtypeStruct((groups, each, rows), BF16),
        in_specs=[VMEM],
        out_specs=VMEM,
        scratch_shapes=[scratch, scratch, scratch],
        name="conv",
    )(got)
    back = lax.all_to_all(conv, "seq", split_axis=0, concat_axis=0, tiled=True)
    mixed, rounded, squares = pl.pallas_call(
        mix_kernel,
        out_shape=(
            jax.ShapeDtypeStruct((rows, channels), F32),
            jax.ShapeDtypeStruct((rows, channels), BF16),
            jax.ShapeDtypeStruct((1, rows), F32),
        ),
        in_specs=[VMEM] * 6,
        out_specs=(VMEM, VMEM, VMEM),
        scratch_shapes=[padded],
        name="mix",
    )(back, q_proj, halo, feat_filter, gated, skip_bias.reshape(1, channels))
    squares = lax.all_gather(squares, "ch")
    normed = pl.pallas_call(
        lambda *refs: norm_kernel(float(columns * channels), *refs),
        out_shape=jax.ShapeDtypeStruct((rows, channels), BF16),
        in_specs=[VMEM] * 3,
        out_specs=VMEM,
        name="norm",
    )(squares, mixed, norm_gain.reshape(1, channels))
    return (rounded, normed)


def solution(mesh):
    return jax.shard_map(
        shards,
        mesh=mesh,
        in_specs=(
            P("seq", "ch"),
            P("seq", "ch"),
            P("seq", "ch"),
            P(None, None, "ch"),
            P("seq", "ch"),
            P("ch"),
            P("ch"),
        ),
        out_specs=(P("seq", "ch"), P("seq", "ch")),
        check_vma=False,
    )
```

time: 199 us -> 102 us (0.51)
  waiting for transfers between devices: 68.9 us -> 0.78 us
  starting transfers between devices: 31.1 us -> 4.03 us
  Pallas kernels: 0 us -> 17 us
  matrix products: 9.14 us -> 0 us
  local copies, waits for them, and re-layouts: 9.55 us -> 3.36 us
  other arithmetic: 2.94 us -> 0.01 us
    all_to_all x2 -> x0, waiting for transfers between devices: 68.3 us -> none  [the longest x1 50.2 us: shards(): lax.all_to_all(for_sending(spread), 'seq', split_axis=2, concat_axis=3, t...]
    all_to_all x2 -> x0, starting transfers between devices: 27 us -> none  [the longest x1 19.2 us: shards(): lax.all_to_all(signals.astype(jnp.bfloat16), 'seq', split_axis=2, concat_...]
    pallas_call x0 -> x4, Pallas kernels: none -> 17 us  [the longest x1 11 us: shards(): pl.pallas_call(conv_kernel, out_shape=jax.ShapeDtypeStruct((groups, each,...]
    psum x1 -> x0, blocking collectives: 15.8 us -> none  [shards(): squares = lax.psum(jnp.sum(mixed * mixed, axis=1), 'ch')]
    all_gather x0 -> x1, blocking collectives: none -> 14.8 us  [shards(): squares = lax.all_gather(squares, 'ch')]
    dot_general x12 -> x0, matrix products: 9.14 us -> none  [contract(): return jnp.einsum(pattern, table, values, precision=highest_precision)]
    another operation x3 -> x0, local copies, waits for them, and re-layouts: 3.54 us -> none  [the longest x1 2.07 us: shards(): spread = jnp.stack([real_part, imag_part], axis=1)]
  transfers between devices with their start and end apart: 3 -> 1, of which waited for: 3 -> 1; matrix products, arithmetic and copies ran while one was open for 0% -> 0% of each run, Pallas kernels for 0% -> 0%
where the time goes in v1:
time: 102 us; the launch traced here: 101 us
  blocking collectives  75.4 us (74%)
  Pallas kernels  17 us (17%)
  starting transfers between devices  4.03 us (4%)
  local copies, waits for them, and re-layouts  3.36 us (3%)
    all_to_all x1, blocking collectives, shards(): got = lax.all_to_all(sent, 'seq', split_axis=0, concat_axis=0, tiled=True)  37.9 us
    all_to_all x1, blocking collectives, shards(): back = lax.all_to_all(conv, 'seq', split_axis=0, concat_axis=0, tiled=True)  22.7 us
    all_gather x1, blocking collectives, shards(): squares = lax.all_gather(squares, 'ch')  14.8 us
    pallas_call x1, Pallas kernels, shards(): pl.pallas_call(conv_kernel, out_shape=jax.ShapeDtypeStruct((groups, each,...  11 us
    ppermute x1, starting transfers between devices, shards(): halo = lax.ppermute(tail, 'seq', [(i, i + 1) for i in range(groups - 1)])  4.03 us
    pallas_call x1, Pallas kernels, shards(): pl.pallas_call(before_kernel, out_shape=(jax.ShapeDtypeStruct((groups, 2...  2.19 us
    slice x3, local copies, waits for them, and re-layouts, shards(): a[rows - (taps - 1):, :]  2.11 us
  transfers between devices with their start and end apart: 1, of which 1 were waited for; matrix products, arithmetic and copies ran while one was open for 0% of the time, Pallas kernels for 0%

profile of v1, /device:TPU:1, one launch (start us, length us, event | category | flops | bytes accessed | tf_op | source)
XLA Modules:
  0.0 101.3 jit_solution(2175000862813452398)
XLA Ops:
  0.6 0.7 slice.9
  1.3 0.7 slice.10
  2.0 0.7 slice.11
  2.8 4.0 %collective-permute-start = (bf16[6,512]{1,0:T(8,128)(2,1)S(1)}, bf16[6,512]{1,0:T(8,128)(2,1)S(1)}, u32[]{:S(2)}, u32[]{:S(2)}) collective-permute-start(bf16[6,512]{1,0:T(8,128)(2,1)S(1)} %pad_maximum_fusion), channel_id=1, source_target_pairs={{0,8},{8,16},{16,24},{24,32},{32,40},{40,48},{48,56},{56,64},{64,7... | collective-permute-start | bytes 18440 | tf_op jit(solution)/shard_map/ppermute | solution.py:121
  6.8 0.8 collective-permute-done.halo_ref
  7.6 0.0 copy-start
  7.6 0.6 copy-done
  8.2 2.2 %before.1 = (bf16[64,16,128]{2,1,0:T(8,128)(2,1)}, f32[128,512]{1,0:T(8,128)}) custom-call(bf16[128,512]{1,0:T(8,128)(2,1)} %k_ref.1, bf16[128,512]{1,0:T(8,128)(2,1)} %v_ref.1, bf16[6,512]{1,0:T(8,128)(2,1)} %copy-done, f32[3,3,512]{2,1,0:T(4,128)} %taps_ref.3, f32[128,512]{1,0:T(8,128)} %filter_ref.1), custom_call_target="tpu_custom_call" | custom-call | tf_op jit(solution)/shard_map/before/pallas_call | solution.py:123
  10.3 37.9 %all_to_all.10.got_ref = bf16[64,16,128]{2,1,0:T(8,128)(2,1)} all-to-all(bf16[64,16,128]{2,1,0:T(8,128)(2,1)} %get-tuple-element.7), channel_id=1, replica_groups=mesh['seq'=64,'ch'=8] {'seq'}, dimensions={0} | all-to-all | bytes 524288 | tf_op jit(solution)/shard_map/all_to_all | solution.py:134
  48.2 11.0 %conv.1 = bf16[64,8,128]{2,1,0:T(8,128)(2,1)} custom-call(bf16[64,16,128]{2,1,0:T(8,128)(2,1)} %all_to_all.10.got_ref), custom_call_target="tpu_custom_call" | custom-call | tf_op jit(solution)/shard_map/conv/pallas_call | solution.py:136
  59.2 22.7 %all_to_all.11.back_ref = bf16[64,8,128]{2,1,0:T(8,128)(2,1)} all-to-all(bf16[64,8,128]{2,1,0:T(8,128)(2,1)} %conv.1), channel_id=1, replica_groups=mesh['seq'=64,'ch'=8] {'seq'}, dimensions={0} | all-to-all | bytes 262144 | tf_op jit(solution)/shard_map/all_to_all | solution.py:144
  82.0 2.0 %mix.1 = (f32[128,512]{1,0:T(8,128)}, bf16[128,512]{1,0:T(8,128)(2,1)}, f32[1,128]{1,0:T(1,128)}) custom-call(bf16[64,8,128]{2,1,0:T(8,128)(2,1)} %all_to_all.11.back_ref, bf16[128,512]{1,0:T(8,128)(2,1)} %q_ref.1, bf16[6,512]{1,0:T(8,128)(2,1)} %copy-done, f32[3,3,512]{2,1,0:T(4,128)} %taps_ref.3, f32[128,512]{1,0:T(8,128)} %get-tuple-element.8.gated_ref, ...), custom_call_target="tpu_custom_call" | custom-call | tf_op jit(solution)/shard_map/mix/pallas_call | solution.py:145
  84.0 0.0 copy-start.1
  84.0 0.7 copy-done.1
  84.7 14.8 %all-gather.1.refs_0_ = f32[8,1,128]{2,1,0:T(1,128)} all-gather(f32[1,1,128]{2,1,0:T(1,128)S(1)} %bitcast.5), channel_id=2, replica_groups=mesh['seq'=64,'ch'=8] {'ch'}, dimensions={0}, use_global_device_ids=true | all-gather | bytes 4608 | tf_op jit(solution)/shard_map/all_gather | solution.py:157
  99.5 1.8 %norm.1 = bf16[128,512]{1,0:T(8,128)(2,1)} custom-call(f32[8,1,128]{2,1,0:T(1,128)} %all-gather.1.refs_0_, f32[128,512]{1,0:T(8,128)} %get-tuple-element.11.refs_1_, f32[1,512]{1,0:T(1,128)} %bitcast.4), custom_call_target="tpu_custom_call" | custom-call | tf_op jit(solution)/shard_map/norm/pallas_call | solution.py:158
  (1 shorter events, 0.0 us)
Async XLA Ops:
  2.8 4.8 %collective-permute-start = (bf16[6,512]{1,0:T(8,128)(2,1)S(1)}, bf16[6,512]{1,0:T(8,128)(2,1)S(1)}, u32[]{:S(2)}, u32[]{:S(2)}) collective-permute-start(bf16[6,512]{1,0:T(8,128)(2,1)S(1)} %pad_maximum_fusion), channel_id=1, source_target_pairs={{0,8},{8,16},{16,24},{24,32},{32,40},{40,48},{48,56},{56,64},{64,7... | collective-permute-start | bytes 18440 | tf_op jit(solution)/shard_map/ppermute | solution.py:121
  7.6 0.6 copy-start
  84.0 0.7 copy-start.1

commit v2 on v1

v2 whole, which is shorter than its diff:
```python
import jax
import jax.numpy as jnp
from jax import lax
from jax.experimental import pallas as pl
from jax.experimental.pallas import tpu as pltpu
from jax.sharding import PartitionSpec as P

EPS = 1e-05
F32 = jnp.float32
BF16 = jnp.bfloat16
VMEM = pl.BlockSpec(memory_space=pltpu.VMEM)
PARAMS = pltpu.CompilerParams(vmem_limit_bytes=16 * 2**20)
STEP = 32
SPAN = 4


def tail_kernel(q_ref, k_ref, v_ref, out_ref):
    ends = [ref[...].astype(F32)[-2:] for ref in (q_ref, k_ref, v_ref)]
    out_ref[...] = jnp.concatenate(ends, axis=0).astype(BF16)


def featured(stream_ref, halo, taps_ref, stream, padded):
    rows = stream_ref.shape[0]
    block = stream_ref[...].astype(F32)
    padded[8:, :] = block
    padded[6:8, :] = halo.astype(F32)
    out = taps_ref[stream, 0:1, :] * block
    out = out + taps_ref[stream, 1:2, :] * padded[7 : 7 + rows, :]
    return out + taps_ref[stream, 2:3, :] * padded[6 : 6 + rows, :]


def early_kernel(filter_ref, bias_ref, gain_ref, taps_ref, kept_bias_ref, kept_gain_ref):
    rows = filter_ref.shape[0]
    groups, each, _ = taps_ref.shape
    down = lax.broadcasted_iota(jnp.int32, (rows, rows), 0)
    across = lax.broadcasted_iota(jnp.int32, (rows, rows), 1)
    backwards = (down + across == rows - 1).astype(BF16)
    taps = jnp.dot(backwards, filter_ref[...].astype(BF16), preferred_element_type=F32)
    taps_ref[...] = taps.T.reshape(groups, each, rows)
    kept_bias_ref[...] = bias_ref[...]
    kept_gain_ref[...] = gain_ref[...]


def before_kernel(k_ref, v_ref, halo_ref, taps_ref, filter_ref, bias_ref, sent_ref, direct_ref, padded):
    rows, channels = k_ref.shape
    groups = sent_ref.shape[0]
    key = featured(k_ref, halo_ref[2:4, :], taps_ref, 1, padded)
    value = featured(v_ref, halo_ref[4:6, :], taps_ref, 2, padded)
    gated = key * value
    direct_ref[...] = bias_ref[...] * gated
    signal = gated.T.reshape(groups, channels // groups, rows)
    sent_ref[...] = jnp.concatenate([signal, filter_ref[...]], axis=1).astype(BF16)


def conv_kernel(got_ref, out_ref, signal, taps, result, *toeplitz_refs):
    blocks, both, size = got_ref.shape
    each = both // 2
    step = STEP
    phases = size // step
    span = SPAN
    reach = span * size
    products = blocks // span
    pair = size // blocks
    got = got_ref[...].astype(F32)
    signal[...] = got[:, :each, :].reshape(blocks * each, size)
    taps[...] = got[:, each:, :].reshape(blocks * each, size)
    row = lax.broadcasted_iota(jnp.int32, (step, size), 0)
    lane = lax.broadcasted_iota(jnp.int32, (step, size), 1)
    own = lane < row + (size + 1 - step)
    column = lane % blocks
    token_column = lax.broadcasted_iota(jnp.int32, (size, size), 1) % blocks
    left = lax.broadcasted_iota(jnp.int32, (reach, size), 1) < blocks

    def windows_of(c):
        now = signal[pl.ds(c, blocks, stride=each), :]
        now = jnp.concatenate([now] * pair, axis=0).T
        past = [now]
        for i in range(1, span + 1):
            past.append(jnp.where(token_column >= i, pltpu.roll(now, i, 1), 0.0))
        past = jnp.concatenate(past[::-1], axis=0)
        halves = []
        for w in range(0, phases, 2):
            start = step * w + step
            halves.append(jnp.where(left, past[start : start + reach], past[start + step : start + step + reach]))
        return jnp.concatenate(halves, axis=1).astype(BF16)

    def fill(c, toeplitz_ref):
        before = jnp.zeros((step, size), F32)
        for d in range(blocks):
            spread = jnp.broadcast_to(taps[pl.ds(each * d + c, 1), :], (step, size))
            turned = pltpu.roll(spread, size + 1 - step, 1, stride=1, stride_axis=0)
            g, back = divmod(d, span)
            at = size * (span - 1 - back)
            toeplitz_ref[step * g : step * g + step, at : at + size] = jnp.where(own, turned, before).astype(BF16)
            before = turned

    def finish(c, toeplitz_ref, windows):
        totals = [jnp.zeros((step, size), F32) for _ in range(phases // 2)]
        rows = toeplitz_ref.shape[0] // 2
        for part in range(2):
            product = jnp.dot(toeplitz_ref[rows * part : rows * part + rows, :], windows, preferred_element_type=F32)
            for i in range(products // 2):
                moved = span * (products // 2 * part + i)
                for h in range(phases // 2):
                    term = product[step * i : step * i + step, size * h : size * h + size]
                    if moved:
                        term = jnp.where(column >= moved, pltpu.roll(term, moved, 1), 0.0)
                    totals[h] = totals[h] + term
        turned_back = jnp.concatenate(totals, axis=1).T
        result[pl.ds(c, blocks, stride=each), :] = jnp.concatenate(
            [turned_back[blocks * w : blocks * w + blocks] for w in range(phases)], axis=1
        )

    def channels(i, carry):
        several = len(toeplitz_refs)
        windows = []
        for k in range(several):
            windows.append(windows_of(several * i + k))
            fill(several * i + k, toeplitz_refs[k])
        for k in range(several):
            finish(several * i + k, toeplitz_refs[k], windows[k])
        return carry

    lax.fori_loop(0, each // len(toeplitz_refs), channels, 0)
    out_ref[...] = result[...].reshape(blocks, each, size).astype(BF16)


def mix_kernel(back_ref, q_ref, halo_ref, taps_ref, direct_ref, mixed_ref, rounded_ref, squares_ref, padded):
    rows, channels = q_ref.shape
    query = featured(q_ref, halo_ref[0:2, :], taps_ref, 0, padded)
    long_conv = back_ref[...].astype(F32).reshape(channels, rows).T
    mixed = query * (long_conv + direct_ref[...])
    mixed_ref[...] = mixed
    rounded_ref[...] = mixed.astype(BF16)
    sums = jnp.sum(mixed * mixed, axis=1, keepdims=True)
    squares_ref[...] = jnp.broadcast_to(sums, (rows, rows)).T[0:1, :]


def norm_kernel(total, squares_ref, mixed_ref, gain_ref, out_ref):
    rows = mixed_ref.shape[0]
    squares = jnp.sum(squares_ref[...], axis=0)
    scale = lax.rsqrt(squares / total + EPS)
    scale = jnp.broadcast_to(scale, (rows, rows)).T[:, 0:1]
    out_ref[...] = (mixed_ref[...] * scale * gain_ref[...]).astype(BF16)


def shards(q_proj, k_proj, v_proj, feat_filter, long_filter, skip_bias, norm_gain):
    rows, channels = q_proj.shape
    taps = feat_filter.shape[1]
    groups = lax.axis_size("seq")
    columns = lax.axis_size("ch")
    each = channels // groups
    last = pl.BlockSpec((16, channels), lambda i: (rows // 16 - 1, 0))
    tail = pl.pallas_call(
        tail_kernel,
        grid=(1,),
        out_shape=jax.ShapeDtypeStruct((3 * (taps - 1), channels), BF16),
        in_specs=[last] * 3,
        out_specs=pl.BlockSpec((3 * (taps - 1), channels), lambda i: (0, 0)),
        compiler_params=pltpu.CompilerParams(vmem_limit_bytes=60 * 2**20),
        name="tail",
    )(q_proj, k_proj, v_proj)
    halo = lax.ppermute(tail, "seq", [(i, i + 1) for i in range(groups - 1)])
    padded = pltpu.VMEM((rows + 8, channels), F32)
    row = jax.ShapeDtypeStruct((1, channels), F32)
    kept_filter, kept_bias, kept_gain = pl.pallas_call(
        early_kernel,
        out_shape=(jax.ShapeDtypeStruct((groups, each, rows), F32), row, row),
        in_specs=[VMEM] * 3,
        out_specs=(VMEM,) * 3,
        cost_estimate=pl.CostEstimate(flops=2 * rows * rows * channels, bytes_accessed=8 * rows * channels, transcendentals=0),
        compiler_params=PARAMS,
        name="early",
    )(long_filter, skip_bias.reshape(1, channels), norm_gain.reshape(1, channels))
    sent, direct = pl.pallas_call(
        before_kernel,
        out_shape=(
            jax.ShapeDtypeStruct((groups, 2 * each, rows), BF16),
            jax.ShapeDtypeStruct((rows, channels), F32),
        ),
        in_specs=[VMEM] * 6,
        out_specs=(VMEM, VMEM),
        scratch_shapes=[padded],
        compiler_params=PARAMS,
        name="before",
    )(k_proj, v_proj, halo, feat_filter, kept_filter, kept_bias)
    got = lax.all_to_all(sent, "seq", split_axis=0, concat_axis=0, tiled=True)
    scratch = pltpu.VMEM((groups * each, rows), F32)
    conv = pl.pallas_call(
        conv_kernel,
        out_shape=jax.ShapeDtypeStruct((groups, each, rows), BF16),
        in_specs=[VMEM],
        out_specs=VMEM,
        scratch_shapes=[scratch] * 3 + [pltpu.VMEM((STEP * groups // SPAN, SPAN * rows), BF16)] * 2,
        compiler_params=PARAMS,
        name="conv",
    )(got)
    back = lax.all_to_all(conv, "seq", split_axis=0, concat_axis=0, tiled=True)
    mixed, rounded, squares = pl.pallas_call(
        mix_kernel,
        out_shape=(
            jax.ShapeDtypeStruct((rows, channels), F32),
            jax.ShapeDtypeStruct((rows, channels), BF16),
            jax.ShapeDtypeStruct((1, rows), F32),
        ),
        in_specs=[VMEM] * 5,
        out_specs=(VMEM, VMEM, VMEM),
        scratch_shapes=[padded],
        compiler_params=PARAMS,
        name="mix",
    )(back, q_proj, halo, feat_filter, direct)
    squares = lax.all_gather(squares, "ch")
    normed = pl.pallas_call(
        lambda *refs: norm_kernel(float(columns * channels), *refs),
        out_shape=jax.ShapeDtypeStruct((rows, channels), BF16),
        in_specs=[VMEM] * 3,
        out_specs=VMEM,
        compiler_params=PARAMS,
        name="norm",
    )(squares, mixed, kept_gain)
    return (rounded, normed)


def solution(mesh):
    return jax.shard_map(
        shards,
        mesh=mesh,
        in_specs=(
            P("seq", "ch"),
            P("seq", "ch"),
            P("seq", "ch"),
            P(None, None, "ch"),
            P("seq", "ch"),
            P("ch"),
            P("ch"),
        ),
        out_specs=(P("seq", "ch"), P("seq", "ch")),
        check_vma=False,
    )
```

time: 102 us -> 88.6 us (0.87)
  Pallas kernels: 17 us -> 8.34 us
  local copies, waits for them, and re-layouts: 3.36 us -> 0.04 us
    pallas_call x1, Pallas kernels: 11 us -> 4.7 us  [shards(): pl.pallas_call(conv_kernel, out_shape=jax.ShapeDtypeStruct((groups, each,...]
    slice x3 -> x0, local copies, waits for them, and re-layouts: 2.11 us -> none  [shards(): a[rows - (taps - 1):, :]]
    pallas_call x1, Pallas kernels: 2.19 us -> 0.31 us  [shards(): pl.pallas_call(before_kernel, out_shape=(jax.ShapeDtypeStruct((groups, 2...]
    pallas_call x0 -> x2, Pallas kernels: none -> 1.67 us  [the longest x1 1.4 us: shards(): pl.pallas_call(tail_kernel, grid=(1,), out_shape=jax.ShapeDtypeStruct((3...]
    pallas_call x1, Pallas kernels: 2.03 us -> 0.82 us  [shards(): pl.pallas_call(mix_kernel, out_shape=(jax.ShapeDtypeStruct((rows, channel...]
    unnamed x4 -> x14, local copies, waits for them, and re-layouts: 1.25 us -> 0.04 us
where the time goes in v2:
time: 88.6 us; the launch traced here: 88.3 us
  blocking collectives  74.4 us (84%)
  Pallas kernels  8.34 us (9%)
  starting transfers between devices  4.15 us (5%)
    all_to_all x1, blocking collectives, shards(): got = lax.all_to_all(sent, 'seq', split_axis=0, concat_axis=0, tiled=True)  37.6 us
    all_to_all x1, blocking collectives, shards(): back = lax.all_to_all(conv, 'seq', split_axis=0, concat_axis=0, tiled=True)  22.5 us
    all_gather x1, blocking collectives, shards(): squares = lax.all_gather(squares, 'ch')  14.3 us
    pallas_call x1, Pallas kernels, shards(): pl.pallas_call(conv_kernel, out_shape=jax.ShapeDtypeStruct((groups, each,...  4.7 us
    ppermute x1, starting transfers between devices, shards(): halo = lax.ppermute(tail, 'seq', [(i, i + 1) for i in range(groups - 1)])  4.15 us
  transfers between devices with their start and end apart: 1, of which 1 were waited for; matrix products, arithmetic and copies ran while one was open for 0% of the time, Pallas kernels for 0%

profile of v2, /device:TPU:1, one launch (start us, length us, event | category | flops | bytes accessed | tf_op | source)
XLA Modules:
  0.0 88.3 jit_solution(11566260575305443305)
XLA Ops:
  0.6 0.0 copy-start.3
  0.6 0.0 copy-start.6
  0.7 0.0 copy-start.4
  0.7 1.4 %tail.1 = bf16[6,512]{1,0:T(8,128)(2,1)} custom-call(bf16[128,512]{1,0:T(8,128)(2,1)} %q_ref.3, bf16[128,512]{1,0:T(8,128)(2,1)} %k_ref.3, bf16[128,512]{1,0:T(8,128)(2,1)} %v_ref.3), custom_call_target="tpu_custom_call" | custom-call | tf_op jit(solution)/shard_map/tail/pallas_call | solution.py:154
  2.1 0.0 copy-start.5
  2.1 4.1 %collective-permute-start = (bf16[6,512]{1,0:T(8,128)(2,1)}, bf16[6,512]{1,0:T(8,128)(2,1)S(1)}, u32[]{:S(2)}, u32[]{:S(2)}) collective-permute-start(bf16[6,512]{1,0:T(8,128)(2,1)} %tail.1), channel_id=1, source_target_pairs={{0,8},{8,16},{16,24},{24,32},{32,40},{40,48},{48,56},{56,64},{64,7... | collective-permute-start | bytes 18440 | tf_op jit(solution)/shard_map/ppermute | solution.py:163
  6.2 0.0 copy-done.3
  6.2 0.0 copy-done.6
  6.2 0.0 copy-done.5
  6.2 0.0 copy-start
  6.3 0.0 copy-start.1
  6.3 0.3 early.1
  6.5 0.7 collective-permute-done.halo_ref
  7.2 0.0 copy-done.4
  7.2 0.0 copy-done
  7.2 0.0 copy-done.1
  7.2 0.3 before.1
  7.5 37.6 %all_to_all.10.got_ref = bf16[64,16,128]{2,1,0:T(8,128)(2,1)S(1)} all-to-all(bf16[64,16,128]{2,1,0:T(8,128)(2,1)S(1)} %get-tuple-element.12), channel_id=1, replica_groups=mesh['seq'=64,'ch'=8] {'seq'}, dimensions={0} | all-to-all | bytes 524288 | tf_op jit(solution)/shard_map/all_to_all | solution.py:187
  45.1 4.7 %conv.1 = bf16[64,8,128]{2,1,0:T(8,128)(2,1)S(1)} custom-call(bf16[64,16,128]{2,1,0:T(8,128)(2,1)S(1)} %all_to_all.10.got_ref), custom_call_target="tpu_custom_call" | custom-call | tf_op jit(solution)/shard_map/conv/pallas_call | solution.py:189
  49.8 0.0 copy-start.2
  49.8 22.5 %all_to_all.11.back_ref = bf16[64,8,128]{2,1,0:T(8,128)(2,1)S(1)} all-to-all(bf16[64,8,128]{2,1,0:T(8,128)(2,1)S(1)} %conv.1), channel_id=1, replica_groups=mesh['seq'=64,'ch'=8] {'seq'}, dimensions={0} | all-to-all | bytes 262144 | tf_op jit(solution)/shard_map/all_to_all | solution.py:198
  72.4 0.0 copy-done.2
  72.4 0.8 mix.1
  73.2 14.3 %all-gather.1.refs_0_ = f32[8,1,128]{2,1,0:T(1,128)S(1)} all-gather(f32[1,1,128]{2,1,0:T(1,128)S(1)} %bitcast.5), channel_id=2, replica_groups=mesh['seq'=64,'ch'=8] {'ch'}, dimensions={0}, use_global_device_ids=true | all-gather | bytes 4608 | tf_op jit(solution)/shard_map/all_gather | solution.py:212
  87.5 0.8 norm.1
Async XLA Ops:
  0.6 5.6 %copy-start.3 = (f32[128,512]{1,0:T(8,128)S(1)}, f32[128,512]{1,0:T(8,128)}, u32[]{:S(2)}) copy-start(f32[128,512]{1,0:T(8,128)} %filter_ref.1) | copy-start | bytes 786436
  0.6 5.6 %copy-start.6 = (f32[512]{0:T(512)S(1)}, f32[512]{0:T(512)}, u32[]{:S(2)}) copy-start(f32[512]{0:T(512)} %param.13) | copy-start | bytes 6148
  0.7 6.6 %copy-start.4 = (f32[3,3,512]{2,1,0:T(4,128)S(1)}, f32[3,3,512]{2,1,0:T(4,128)}, u32[]{:S(2)}) copy-start(f32[3,3,512]{2,1,0:T(4,128)} %taps_ref.3) | copy-start | bytes 55300
  2.1 4.2 %copy-start.5 = (f32[512]{0:T(512)S(1)}, f32[512]{0:T(512)}, u32[]{:S(2)}) copy-start(f32[512]{0:T(512)} %param.12) | copy-start | bytes 6148
  2.1 5.1 %collective-permute-start = (bf16[6,512]{1,0:T(8,128)(2,1)}, bf16[6,512]{1,0:T(8,128)(2,1)S(1)}, u32[]{:S(2)}, u32[]{:S(2)}) collective-permute-start(bf16[6,512]{1,0:T(8,128)(2,1)} %tail.1), channel_id=1, source_target_pairs={{0,8},{8,16},{16,24},{24,32},{32,40},{40,48},{48,56},{56,64},{64,7... | collective-permute-start | bytes 18440 | tf_op jit(solution)/shard_map/ppermute | solution.py:163
  6.2 1.0 %copy-start = (bf16[128,512]{1,0:T(8,128)(2,1)S(1)}, bf16[128,512]{1,0:T(8,128)(2,1)}, u32[]{:S(2)}) copy-start(bf16[128,512]{1,0:T(8,128)(2,1)} %k_ref.3) | copy-start | bytes 393220
  6.3 1.0 %copy-start.1 = (bf16[128,512]{1,0:T(8,128)(2,1)S(1)}, bf16[128,512]{1,0:T(8,128)(2,1)}, u32[]{:S(2)}) copy-start(bf16[128,512]{1,0:T(8,128)(2,1)} %v_ref.3) | copy-start | bytes 393220
  49.8 22.6 %copy-start.2 = (bf16[128,512]{1,0:T(8,128)(2,1)S(1)}, bf16[128,512]{1,0:T(8,128)(2,1)}, u32[]{:S(2)}) copy-start(bf16[128,512]{1,0:T(8,128)(2,1)} %q_ref.3) | copy-start | bytes 393220

commit v3 on v2

v3 whole, which is shorter than its diff:
```python
import jax
import jax.numpy as jnp
from jax import lax
from jax.experimental import pallas as pl
from jax.experimental.pallas import tpu as pltpu
from jax.sharding import PartitionSpec as P

EPS = 1e-05
F32 = jnp.float32
BF16 = jnp.bfloat16
VMEM = pl.BlockSpec(memory_space=pltpu.VMEM)
HBM = pl.BlockSpec(memory_space=pltpu.HBM)
PARAMS = pltpu.CompilerParams(vmem_limit_bytes=16 * 2**20)
STEP = 32
SPAN = 4


def shift_down(block, count):
    return jnp.concatenate([jnp.zeros((count, block.shape[1]), block.dtype), block[:-count]], axis=0)


def inside(stream_ref, taps_ref, stream, padded):
    rows = stream_ref.shape[0]
    block = stream_ref[...].astype(F32)
    padded[8:, :] = block
    padded[6:8, :] = jnp.zeros((2, block.shape[1]), F32)
    out = taps_ref[stream, 0:1, :] * block
    out = out + taps_ref[stream, 1:2, :] * padded[7 : 7 + rows, :]
    return out + taps_ref[stream, 2:3, :] * padded[6 : 6 + rows, :]


def into_next(stream_ref, taps_ref, stream):
    last = stream_ref[stream_ref.shape[0] - 16 :, :].astype(F32)[14:]
    first = taps_ref[stream, 1:2, :] * last[1:] + taps_ref[stream, 2:3, :] * last[:1]
    return [first, taps_ref[stream, 2:3, :] * last[1:]]


def before_kernel(*refs):
    sources, (sent_ref, kept_gain_ref, padded, *kept, sems) = refs[:7], refs[7:]
    loads = [pltpu.make_async_copy(a, b, sems.at[i]) for i, (a, b) in enumerate(zip(sources, kept, strict=True))]
    for load in loads:
        load.start()
    q_ref, k_ref, v_ref, taps_ref, filter_ref, bias_ref, gain_ref = kept
    for load in loads:
        load.wait()
    rows, channels = k_ref.shape
    groups = sent_ref.shape[0]
    each = channels // groups
    key = inside(k_ref, taps_ref, 1, padded)
    value = inside(v_ref, taps_ref, 2, padded)
    signal = (key * value).T.reshape(groups, each, rows)
    down = lax.broadcasted_iota(jnp.int32, (rows, rows), 0)
    across = lax.broadcasted_iota(jnp.int32, (rows, rows), 1)
    backwards = (down + across == rows - 1).astype(BF16)
    taps = jnp.dot(backwards, filter_ref[...].astype(BF16), preferred_element_type=F32)
    taps = taps.T.reshape(groups, each, rows)
    start = q_ref[0:16, :].astype(F32)[0:2]
    first = taps_ref[0, 0:1, :] * start
    second = taps_ref[0, 1:2, :] * start[0:1]
    high = bias_ref[...].astype(BF16).astype(F32)
    middle = (bias_ref[...] - high).astype(BF16).astype(F32)
    low = bias_ref[...] - high - middle
    edge = [key[0:2], value[0:2], first[0:1], first[1:2] + second, jnp.zeros((2, channels), F32)]
    for stream, ref in ((1, k_ref), (2, v_ref), (0, q_ref)):
        edge += into_next(ref, taps_ref, stream)
    edge += [jnp.zeros((2, channels), F32), high, middle, low, jnp.zeros((rows - 19, channels), F32)]
    edge = jnp.concatenate(edge, axis=0).T.reshape(groups, each, rows)
    sent_ref[...] = jnp.concatenate([signal, taps, edge], axis=1).astype(BF16)
    kept_gain_ref[...] = gain_ref[...]


def conv_kernel(got_ref, out_ref, signal, taps, edges, result, *toeplitz_refs):
    blocks, kinds, size = got_ref.shape
    each = kinds // 3
    step = STEP
    phases = size // step
    span = SPAN
    reach = span * size
    products = blocks // span
    pair = size // blocks
    got = got_ref[...].astype(F32)
    signal[...] = got[:, :each, :].reshape(blocks * each, size)
    taps[...] = got[:, each : 2 * each, :].reshape(blocks * each, size)
    edge = got[:, 2 * each :, :].reshape(blocks * each, size)
    edge = edge + pltpu.roll(shift_down(edge, each), size - 8, 1)
    place = lax.broadcasted_iota(jnp.int32, edge.shape, 1)
    signal[...] = jnp.where(place < 2, edge * pltpu.roll(edge, size - 2, 1), signal[...])
    edges[...] = edge
    row = lax.broadcasted_iota(jnp.int32, (step, size), 0)
    lane = lax.broadcasted_iota(jnp.int32, (step, size), 1)
    own = lane < row + (size + 1 - step)
    column = lane % blocks
    place = lax.broadcasted_iota(jnp.int32, (blocks, size), 1)
    start = place < 2
    parts = (place[0:1, :] >= 16) & (place[0:1, :] < 19)
    token_column = lax.broadcasted_iota(jnp.int32, (size, size), 1) % blocks
    left = lax.broadcasted_iota(jnp.int32, (reach, size), 1) < blocks

    def windows_of(c):
        now = signal[pl.ds(c, blocks, stride=each), :]
        now = jnp.concatenate([now] * pair, axis=0).T
        past = [now]
        for i in range(1, span + 1):
            past.append(jnp.where(token_column >= i, pltpu.roll(now, i, 1), 0.0))
        past = jnp.concatenate(past[::-1], axis=0)
        halves = []
        for w in range(0, phases, 2):
            start = step * w + step
            halves.append(jnp.where(left, past[start : start + reach], past[start + step : start + step + reach]))
        return jnp.concatenate(halves, axis=1).astype(BF16)

    def fill(c, toeplitz_ref):
        before = jnp.zeros((step, size), F32)
        for d in range(blocks):
            spread = jnp.broadcast_to(taps[pl.ds(each * d + c, 1), :], (step, size))
            turned = pltpu.roll(spread, size + 1 - step, 1, stride=1, stride_axis=0)
            g, back = divmod(d, span)
            at = size * (span - 1 - back)
            toeplitz_ref[step * g : step * g + step, at : at + size] = jnp.where(own, turned, before).astype(BF16)
            before = turned

    def finish(c, toeplitz_ref, windows):
        totals = [jnp.zeros((step, size), F32) for _ in range(phases // 2)]
        rows = toeplitz_ref.shape[0] // 2
        for part in range(2):
            product = jnp.dot(toeplitz_ref[rows * part : rows * part + rows, :], windows, preferred_element_type=F32)
            for i in range(products // 2):
                moved = span * (products // 2 * part + i)
                for h in range(phases // 2):
                    term = product[step * i : step * i + step, size * h : size * h + size]
                    if moved:
                        term = jnp.where(column >= moved, pltpu.roll(term, moved, 1), 0.0)
                    totals[h] = totals[h] + term
        turned_back = jnp.concatenate(totals, axis=1).T
        turned_back = jnp.concatenate([turned_back[blocks * w : blocks * w + blocks] for w in range(phases)], axis=1)
        edge = edges[pl.ds(c, blocks, stride=each), :]
        direct = jnp.sum(jnp.where(parts, edge[0:1, :], 0.0), axis=1, keepdims=True)
        mixed = turned_back + direct * signal[pl.ds(c, blocks, stride=each), :]
        mixed = mixed * jnp.where(start, pltpu.roll(edge, size - 4, 1), 1.0)
        result[pl.ds(c, blocks, stride=each), :] = mixed

    def channels(i, carry):
        several = len(toeplitz_refs)
        windows = []
        for k in range(several):
            windows.append(windows_of(several * i + k))
            fill(several * i + k, toeplitz_refs[k])
        for k in range(several):
            finish(several * i + k, toeplitz_refs[k], windows[k])
        return carry

    lax.fori_loop(0, each // len(toeplitz_refs), channels, 0)
    out_ref[...] = result[...].reshape(blocks, each, size).astype(BF16)


def mix_kernel(back_ref, q_ref, taps_ref, mixed_ref, rounded_ref, squares_ref, padded):
    rows, channels = q_ref.shape
    query = inside(q_ref, taps_ref, 0, padded)
    back = back_ref[...].astype(F32).reshape(channels, rows).T
    row = lax.broadcasted_iota(jnp.int32, (rows, channels), 0)
    mixed = back * jnp.where(row < 2, 1.0, query)
    mixed_ref[...] = mixed
    rounded_ref[...] = mixed.astype(BF16)
    sums = jnp.sum(mixed * mixed, axis=1, keepdims=True)
    squares_ref[...] = jnp.broadcast_to(sums, (rows, rows)).T[0:1, :]


def norm_kernel(total, squares_ref, mixed_ref, gain_ref, out_ref):
    rows = mixed_ref.shape[0]
    squares = jnp.sum(squares_ref[...], axis=0)
    scale = lax.rsqrt(squares / total + EPS)
    scale = jnp.broadcast_to(scale, (rows, rows)).T[:, 0:1]
    out_ref[...] = (mixed_ref[...] * scale * gain_ref[...]).astype(BF16)


def shards(q_proj, k_proj, v_proj, feat_filter, long_filter, skip_bias, norm_gain):
    rows, channels = q_proj.shape
    groups = lax.axis_size("seq")
    columns = lax.axis_size("ch")
    each = channels // groups
    padded = pltpu.VMEM((rows + 8, channels), F32)
    sources = (q_proj, k_proj, v_proj, feat_filter, long_filter, skip_bias.reshape(1, channels), norm_gain.reshape(1, channels))
    sent, kept_gain = pl.pallas_call(
        before_kernel,
        out_shape=(
            jax.ShapeDtypeStruct((groups, 3 * each, rows), BF16),
            jax.ShapeDtypeStruct((1, channels), F32),
        ),
        in_specs=[HBM] * 7,
        out_specs=(VMEM, VMEM),
        scratch_shapes=[padded] + [pltpu.VMEM(a.shape, a.dtype) for a in sources] + [pltpu.SemaphoreType.DMA((7,))],
        compiler_params=PARAMS,
        name="before",
    )(*(pltpu.with_memory_space_constraint(a, pltpu.HBM) for a in sources))
    got = lax.all_to_all(sent, "seq", split_axis=0, concat_axis=0, tiled=True)
    scratch = pltpu.VMEM((groups * each, rows), F32)
    conv = pl.pallas_call(
        conv_kernel,
        out_shape=jax.ShapeDtypeStruct((groups, each, rows), BF16),
        in_specs=[VMEM],
        out_specs=VMEM,
        scratch_shapes=[scratch] * 4 + [pltpu.VMEM((STEP * groups // SPAN, SPAN * rows), BF16)] * 2,
        compiler_params=PARAMS,
        name="conv",
    )(got)
    back = lax.all_to_all(conv, "seq", split_axis=0, concat_axis=0, tiled=True)
    mixed, rounded, squares = pl.pallas_call(
        mix_kernel,
        out_shape=(
            jax.ShapeDtypeStruct((rows, channels), F32),
            jax.ShapeDtypeStruct((rows, channels), BF16),
            jax.ShapeDtypeStruct((1, rows), F32),
        ),
        in_specs=[VMEM] * 3,
        out_specs=(VMEM, VMEM, VMEM),
        scratch_shapes=[padded],
        compiler_params=PARAMS,
        name="mix",
    )(back, q_proj, feat_filter)
    squares = lax.all_gather(squares, "ch")
    normed = pl.pallas_call(
        lambda *refs: norm_kernel(float(columns * channels), *refs),
        out_shape=jax.ShapeDtypeStruct((rows, channels), BF16),
        in_specs=[VMEM] * 3,
        out_specs=VMEM,
        compiler_params=PARAMS,
        name="norm",
    )(squares, mixed, kept_gain)
    return (rounded, normed)


def solution(mesh):
    return jax.shard_map(
        shards,
        mesh=mesh,
        in_specs=(
            P("seq", "ch"),
            P("seq", "ch"),
            P("seq", "ch"),
            P(None, None, "ch"),
            P("seq", "ch"),
            P("ch"),
            P("ch"),
        ),
        out_specs=(P("seq", "ch"), P("seq", "ch")),
        check_vma=False,
    )
```

time: 88.6 us -> 89.4 us (level)
  blocking collectives: 74.4 us -> 80.3 us
  starting transfers between devices: 4.15 us -> 0 us
    all_to_all x1, blocking collectives: 37.6 us -> 44 us  [shards(): got = lax.all_to_all(sent, 'seq', split_axis=0, concat_axis=0, tiled=True)]
    ppermute x1 -> x0, starting transfers between devices: 4.15 us -> none  [shards(): halo = lax.ppermute(tail, 'seq', [(i, i + 1) for i in range(groups - 1)])]
    pallas_call x3 -> x1, Pallas kernels: 1.98 us -> 1.62 us  [shards(): pl.pallas_call(before_kernel, out_shape=(jax.ShapeDtypeStruct((groups, 3...]
  transfers between devices with their start and end apart: 1 -> 0, of which waited for: 1 -> 0; matrix products, arithmetic and copies ran while one was open for 0% -> 0% of each run, Pallas kernels for 0% -> 0%
where the time goes in v3:
time: 89.4 us; the launch traced here: 89.2 us
  blocking collectives  80.3 us (90%)
  Pallas kernels  8.25 us (9%)
    all_to_all x1, blocking collectives, shards(): got = lax.all_to_all(sent, 'seq', split_axis=0, concat_axis=0, tiled=True)  44 us
    all_to_all x1, blocking collectives, shards(): back = lax.all_to_all(conv, 'seq', split_axis=0, concat_axis=0, tiled=True)  22.4 us
    all_gather x1, blocking collectives, shards(): squares = lax.all_gather(squares, 'ch')  13.9 us
    pallas_call x1, Pallas kernels, shards(): pl.pallas_call(conv_kernel, out_shape=jax.ShapeDtypeStruct((groups, each,...  4.98 us

profile of v3, /device:TPU:1, one launch (start us, length us, event | category | flops | bytes accessed | tf_op | source)
XLA Modules:
  0.0 89.2 jit_solution(2273025221088216838)
XLA Ops:
  0.6 1.6 %before.1 = (bf16[64,24,128]{2,1,0:T(8,128)(2,1)S(1)}, f32[1,512]{1,0:T(1,128)S(1)}) custom-call(bf16[128,512]{1,0:T(8,128)(2,1)} %q_ref.1, bf16[128,512]{1,0:T(8,128)(2,1)} %refs_1_.1, bf16[128,512]{1,0:T(8,128)(2,1)} %refs_2_.1, f32[3,3,512]{2,1,0:T(4,128)} %taps_ref.1, f32[128,512]{1,0:T(8,128)} %refs_4_.1, f32[1,512]{1,0:T(1,128)} %bitcast.4, ...), custom_call_target="tpu_custom_call" | custom-call | tf_op jit(solution)/shard_map/before/pallas_call | solution.py:183
  2.3 44.0 %all_to_all.10.got_ref = bf16[64,24,128]{2,1,0:T(8,128)(2,1)S(1)} all-to-all(bf16[64,24,128]{2,1,0:T(8,128)(2,1)S(1)} %get-tuple-element.7), channel_id=1, replica_groups=mesh['seq'=64,'ch'=8] {'seq'}, dimensions={0} | all-to-all | bytes 786432 | tf_op jit(solution)/shard_map/all_to_all | solution.py:195
  46.3 5.0 %conv.1 = bf16[64,8,128]{2,1,0:T(8,128)(2,1)S(1)} custom-call(bf16[64,24,128]{2,1,0:T(8,128)(2,1)S(1)} %all_to_all.10.got_ref), custom_call_target="tpu_custom_call" | custom-call | tf_op jit(solution)/shard_map/conv/pallas_call | solution.py:197
  51.2 0.0 copy-start
  51.3 0.0 copy-start.1
  51.3 22.4 %all_to_all.11.back_ref = bf16[64,8,128]{2,1,0:T(8,128)(2,1)S(1)} all-to-all(bf16[64,8,128]{2,1,0:T(8,128)(2,1)S(1)} %conv.1), channel_id=1, replica_groups=mesh['seq'=64,'ch'=8] {'seq'}, dimensions={0} | all-to-all | bytes 262144 | tf_op jit(solution)/shard_map/all_to_all | solution.py:206
  73.7 0.0 copy-done
  73.7 0.0 copy-done.1
  73.7 0.8 mix.1
  74.5 13.9 %all-gather.1.refs_0_ = f32[8,1,128]{2,1,0:T(1,128)S(1)} all-gather(f32[1,1,128]{2,1,0:T(1,128)S(1)} %bitcast.3), channel_id=2, replica_groups=mesh['seq'=64,'ch'=8] {'ch'}, dimensions={0}, use_global_device_ids=true | all-gather | bytes 4608 | tf_op jit(solution)/shard_map/all_gather | solution.py:220
  88.3 0.8 norm.1
Async XLA Ops:
  51.2 22.4 %copy-start = (bf16[128,512]{1,0:T(8,128)(2,1)S(1)}, bf16[128,512]{1,0:T(8,128)(2,1)}, u32[]{:S(2)}) copy-start(bf16[128,512]{1,0:T(8,128)(2,1)} %q_ref.1) | copy-start | bytes 393220
  51.3 22.4 %copy-start.1 = (f32[3,3,512]{2,1,0:T(4,128)S(1)}, f32[3,3,512]{2,1,0:T(4,128)}, u32[]{:S(2)}) copy-start(f32[3,3,512]{2,1,0:T(4,128)} %taps_ref.1) | copy-start | bytes 55300

commit v4 on v3

--- a/solution.py
+++ b/solution.py
@@ -13,6 +13,8 @@
 PARAMS = pltpu.CompilerParams(vmem_limit_bytes=16 * 2**20)
 STEP = 32
 SPAN = 4
+MESSAGE = 18
+EDGE = 16
 
 
 def shift_down(block, count):
@@ -36,7 +38,7 @@
 
 
 def before_kernel(*refs):
-    sources, (sent_ref, kept_gain_ref, padded, *kept, sems) = refs[:7], refs[7:]
+    sources, (sent_ref, kept_gain_ref, padded, edges, *kept, sems) = refs[:7], refs[7:]
     loads = [pltpu.make_async_copy(a, b, sems.at[i]) for i, (a, b) in enumerate(zip(sources, kept, strict=True))]
     for load in loads:
         load.start()
@@ -44,7 +46,7 @@
     for load in loads:
         load.wait()
     rows, channels = k_ref.shape
-    groups = sent_ref.shape[0]
+    groups = sent_ref.shape[0] // MESSAGE
     each = channels // groups
     key = inside(k_ref, taps_ref, 1, padded)
     value = inside(v_ref, taps_ref, 2, padded)
@@ -60,44 +62,53 @@
     high = bias_ref[...].astype(BF16).astype(F32)
     middle = (bias_ref[...] - high).astype(BF16).astype(F32)
     low = bias_ref[...] - high - middle
-    edge = [key[0:2], value[0:2], first[0:1], first[1:2] + second, jnp.zeros((2, channels), F32)]
+    edge = [key[0:2], value[0:2], first[0:1], first[1:2] + second]
     for stream, ref in ((1, k_ref), (2, v_ref), (0, q_ref)):
         edge += into_next(ref, taps_ref, stream)
-    edge += [jnp.zeros((2, channels), F32), high, middle, low, jnp.zeros((rows - 19, channels), F32)]
-    edge = jnp.concatenate(edge, axis=0).T.reshape(groups, each, rows)
-    sent_ref[...] = jnp.concatenate([signal, taps, edge], axis=1).astype(BF16)
+    edge += [high, middle, low, jnp.zeros((rows - 15, channels), F32)]
+    edges[...] = jnp.concatenate(edge, axis=0).T
+    edge = edges[pl.ds(0, groups, stride=each), :]
+    for c in range(1, each):
+        edge = edge + pltpu.roll(edges[pl.ds(c, groups, stride=each), :], EDGE * c, 1)
+    blank = jnp.zeros((1, rows), F32)
+    messages = []
+    for s in range(groups):
+        messages += [signal[s], taps[s], edge[s : s + 1], blank]
+    sent_ref[...] = jnp.concatenate(messages, axis=0).astype(BF16)
     kept_gain_ref[...] = gain_ref[...]
 
 
-def conv_kernel(got_ref, out_ref, signal, taps, edges, result, *toeplitz_refs):
-    blocks, kinds, size = got_ref.shape
-    each = kinds // 3
+def conv_kernel(got_ref, out_ref, got, signal, edges, result, *toeplitz_refs):
+    blocks, each, size = out_ref.shape
     step = STEP
     phases = size // step
     span = SPAN
     reach = span * size
     products = blocks // span
     pair = size // blocks
-    got = got_ref[...].astype(F32)
-    signal[...] = got[:, :each, :].reshape(blocks * each, size)
-    taps[...] = got[:, each : 2 * each, :].reshape(blocks * each, size)
-    edge = got[:, 2 * each :, :].reshape(blocks * each, size)
-    edge = edge + pltpu.roll(shift_down(edge, each), size - 8, 1)
-    place = lax.broadcasted_iota(jnp.int32, edge.shape, 1)
-    signal[...] = jnp.where(place < 2, edge * pltpu.roll(edge, size - 2, 1), signal[...])
-    edges[...] = edge
+    got[...] = got_ref[...].astype(F32)
     row = lax.broadcasted_iota(jnp.int32, (step, size), 0)
     lane = lax.broadcasted_iota(jnp.int32, (step, size), 1)
     own = lane < row + (size + 1 - step)
     column = lane % blocks
     place = lax.broadcasted_iota(jnp.int32, (blocks, size), 1)
     start = place < 2
-    parts = (place[0:1, :] >= 16) & (place[0:1, :] < 19)
+    parts = (place[0:1, :] >= 12) & (place[0:1, :] < 15)
+    packed = got[pl.ds(2 * each, blocks, stride=MESSAGE), :]
+    for c in range(each):
+        edge = pltpu.roll(packed, size - EDGE * c, 1) if c else packed
+        edge = edge + jnp.where(place < 6, pltpu.roll(shift_down(edge, 1), size - 6, 1), 0.0)
+        own_tokens = got[pl.ds(c, blocks, stride=MESSAGE), :]
+        signal[blocks * c : blocks * c + blocks, :] = jnp.where(start, edge * pltpu.roll(edge, size - 2, 1), own_tokens)
+        edges[blocks * c : blocks * c + blocks, :] = edge
+
+    def rows_of(c):
+        return pl.ds(pl.multiple_of(blocks * c, blocks), blocks)
     token_column = lax.broadcasted_iota(jnp.int32, (size, size), 1) % blocks
     left = lax.broadcasted_iota(jnp.int32, (reach, size), 1) < blocks
 
     def windows_of(c):
-        now = signal[pl.ds(c, blocks, stride=each), :]
+        now = signal[rows_of(c), :]
         now = jnp.concatenate([now] * pair, axis=0).T
         past = [now]
         for i in range(1, span + 1):
@@ -112,7 +123,7 @@
     def fill(c, toeplitz_ref):
         before = jnp.zeros((step, size), F32)
         for d in range(blocks):
-            spread = jnp.broadcast_to(taps[pl.ds(each * d + c, 1), :], (step, size))
+            spread = jnp.broadcast_to(got[pl.ds(MESSAGE * d + each + c, 1), :], (step, size))
             turned = pltpu.roll(spread, size + 1 - step, 1, stride=1, stride_axis=0)
             g, back = divmod(d, span)
             at = size * (span - 1 - back)
@@ -133,9 +144,9 @@
                     totals[h] = totals[h] + term
         turned_back = jnp.concatenate(totals, axis=1).T
         turned_back = jnp.concatenate([turned_back[blocks * w : blocks * w + blocks] for w in range(phases)], axis=1)
-        edge = edges[pl.ds(c, blocks, stride=each), :]
+        edge = edges[rows_of(c), :]
         direct = jnp.sum(jnp.where(parts, edge[0:1, :], 0.0), axis=1, keepdims=True)
-        mixed = turned_back + direct * signal[pl.ds(c, blocks, stride=each), :]
+        mixed = turned_back + direct * signal[rows_of(c), :]
         mixed = mixed * jnp.where(start, pltpu.roll(edge, size - 4, 1), 1.0)
         result[pl.ds(c, blocks, stride=each), :] = mixed
 
@@ -183,23 +194,24 @@
     sent, kept_gain = pl.pallas_call(
         before_kernel,
         out_shape=(
-            jax.ShapeDtypeStruct((groups, 3 * each, rows), BF16),
+            jax.ShapeDtypeStruct((groups * MESSAGE, rows), BF16),
             jax.ShapeDtypeStruct((1, channels), F32),
         ),
         in_specs=[HBM] * 7,
         out_specs=(VMEM, VMEM),
-        scratch_shapes=[padded] + [pltpu.VMEM(a.shape, a.dtype) for a in sources] + [pltpu.SemaphoreType.DMA((7,))],
+        scratch_shapes=[padded, pltpu.VMEM((channels, rows), F32)] + [pltpu.VMEM(a.shape, a.dtype) for a in sources] + [pltpu.SemaphoreType.DMA((7,))],
         compiler_params=PARAMS,
         name="before",
     )(*(pltpu.with_memory_space_constraint(a, pltpu.HBM) for a in sources))
-    got = lax.all_to_all(sent, "seq", split_axis=0, concat_axis=0, tiled=True)
+    sent = sent.reshape(groups, MESSAGE // 2, 2, rows)
+    got = lax.all_to_all(sent, "seq", split_axis=0, concat_axis=0, tiled=True).reshape(groups * MESSAGE, rows)
     scratch = pltpu.VMEM((groups * each, rows), F32)
     conv = pl.pallas_call(
         conv_kernel,
         out_shape=jax.ShapeDtypeStruct((groups, each, rows), BF16),
         in_specs=[VMEM],
         out_specs=VMEM,
-        scratch_shapes=[scratch] * 4 + [pltpu.VMEM((STEP * groups // SPAN, SPAN * rows), BF16)] * 2,
+        scratch_shapes=[pltpu.VMEM((groups * MESSAGE, rows), F32)] + [scratch] * 3 + [pltpu.VMEM((STEP * groups // SPAN, SPAN * rows), BF16)] * 2,
         compiler_params=PARAMS,
         name="conv",
     )(got)

time: 89.4 us -> 85.3 us (0.954)
  blocking collectives: 80.3 us -> 75.9 us
    all_to_all x1, blocking collectives: 44 us -> 39.6 us  [shards(): lax.all_to_all(sent, 'seq', split_axis=0, concat_axis=0, tiled=True)]
where the time goes in v4:
time: 85.3 us; the launch traced here: 85.1 us
  blocking collectives  75.9 us (89%)
  Pallas kernels  8.58 us (10%)
    all_to_all x1, blocking collectives, shards(): lax.all_to_all(sent, 'seq', split_axis=0, concat_axis=0, tiled=True)  39.6 us
    all_to_all x1, blocking collectives, shards(): back = lax.all_to_all(conv, 'seq', split_axis=0, concat_axis=0, tiled=True)  22.4 us
    all_gather x1, blocking collectives, shards(): squares = lax.all_gather(squares, 'ch')  13.9 us
    pallas_call x1, Pallas kernels, shards(): pl.pallas_call(conv_kernel, out_shape=jax.ShapeDtypeStruct((groups, each,...  5.13 us
    pallas_call x1, Pallas kernels, shards(): pl.pallas_call(before_kernel, out_shape=(jax.ShapeDtypeStruct((groups * M...  1.81 us

profile of v4, /device:TPU:1, one launch (start us, length us, event | category | flops | bytes accessed | tf_op | source)
XLA Modules:
  0.0 85.1 jit_solution(2543610952069597104)
XLA Ops:
  0.6 1.8 %before.1 = (bf16[1152,128]{1,0:T(8,128)(2,1)S(1)}, f32[1,512]{1,0:T(1,128)S(1)}) custom-call(bf16[128,512]{1,0:T(8,128)(2,1)} %q_ref.1, bf16[128,512]{1,0:T(8,128)(2,1)} %refs_1_.1, bf16[128,512]{1,0:T(8,128)(2,1)} %refs_2_.1, f32[3,3,512]{2,1,0:T(4,128)} %taps_ref.1, f32[128,512]{1,0:T(8,128)} %refs_4_.1, f32[1,512]{1,0:T(1,128)} %bitcast.8, f32[1,512]{1,0:T(1,128)} %bitcast.9), custom_call_target="tpu_custom_call" | custom-call | tf_op jit(solution)/shard_map/before/pallas_call | solution.py:194
  2.4 39.6 %all_to_all.10 = bf16[64,9,2,128]{3,2,1,0:T(2,128)(2,1)S(1)} all-to-all(bf16[64,9,2,128]{3,2,1,0:T(2,128)(2,1)S(1)} %bitcast.6), channel_id=1, replica_groups=mesh['seq'=64,'ch'=8] {'seq'}, dimensions={0} | all-to-all | bytes 589824 | tf_op jit(solution)/shard_map/all_to_all | solution.py:207
  42.0 5.1 %conv.1 = bf16[64,8,128]{2,1,0:T(8,128)(2,1)S(1)} custom-call(bf16[1152,128]{1,0:T(8,128)(2,1)S(1)} %bitcast.5), custom_call_target="tpu_custom_call" | custom-call | tf_op jit(solution)/shard_map/conv/pallas_call | solution.py:209
  47.1 0.0 copy-start
  47.2 0.0 copy-start.1
  47.2 22.4 %all_to_all.11.back_ref = bf16[64,8,128]{2,1,0:T(8,128)(2,1)S(1)} all-to-all(bf16[64,8,128]{2,1,0:T(8,128)(2,1)S(1)} %conv.1), channel_id=1, replica_groups=mesh['seq'=64,'ch'=8] {'seq'}, dimensions={0} | all-to-all | bytes 262144 | tf_op jit(solution)/shard_map/all_to_all | solution.py:218
  69.6 0.0 copy-done
  69.6 0.0 copy-done.1
  69.6 0.8 mix.1
  70.4 13.9 %all-gather.1.refs_0_ = f32[8,1,128]{2,1,0:T(1,128)S(1)} all-gather(f32[1,1,128]{2,1,0:T(1,128)S(1)} %bitcast.7), channel_id=2, replica_groups=mesh['seq'=64,'ch'=8] {'ch'}, dimensions={0}, use_global_device_ids=true | all-gather | bytes 4608 | tf_op jit(solution)/shard_map/all_gather | solution.py:232
  84.3 0.8 norm.1
Async XLA Ops:
  47.1 22.5 %copy-start = (bf16[128,512]{1,0:T(8,128)(2,1)S(1)}, bf16[128,512]{1,0:T(8,128)(2,1)}, u32[]{:S(2)}) copy-start(bf16[128,512]{1,0:T(8,128)(2,1)} %q_ref.1) | copy-start | bytes 393220
  47.2 22.4 %copy-start.1 = (f32[3,3,512]{2,1,0:T(4,128)S(1)}, f32[3,3,512]{2,1,0:T(4,128)}, u32[]{:S(2)}) copy-start(f32[3,3,512]{2,1,0:T(4,128)} %taps_ref.1) | copy-start | bytes 55300

commit v5 on v4

v5 whole, which is shorter than its diff:
```python
import jax
import jax.numpy as jnp
from jax import lax
from jax.experimental import pallas as pl
from jax.experimental.pallas import tpu as pltpu
from jax.sharding import PartitionSpec as P

EPS = 1e-05
F32 = jnp.float32
BF16 = jnp.bfloat16
VMEM = pl.BlockSpec(memory_space=pltpu.VMEM)
HBM = pl.BlockSpec(memory_space=pltpu.HBM)
PARAMS = pltpu.CompilerParams(vmem_limit_bytes=16 * 2**20)
STEP = 32
SPAN = 4
MESSAGE = 18
EDGE = 16
TOGETHER = 4


def shift_down(block, count):
    return jnp.concatenate([jnp.zeros((count, block.shape[1]), block.dtype), block[:-count]], axis=0)


def inside(stream_ref, taps_ref, stream, padded):
    rows = stream_ref.shape[0]
    block = stream_ref[...].astype(F32)
    padded[8:, :] = block
    padded[6:8, :] = jnp.zeros((2, block.shape[1]), F32)
    out = taps_ref[stream, 0:1, :] * block
    out = out + taps_ref[stream, 1:2, :] * padded[7 : 7 + rows, :]
    return out + taps_ref[stream, 2:3, :] * padded[6 : 6 + rows, :]


def into_next(stream_ref, taps_ref, stream):
    last = stream_ref[stream_ref.shape[0] - 16 :, :].astype(F32)[14:]
    first = taps_ref[stream, 1:2, :] * last[1:] + taps_ref[stream, 2:3, :] * last[:1]
    return [first, taps_ref[stream, 2:3, :] * last[1:]]


def before_kernel(*refs):
    sources, (sent_ref, kept_gain_ref, padded, edges, *kept, sems) = refs[:7], refs[7:]
    loads = [pltpu.make_async_copy(a, b, sems.at[i]) for i, (a, b) in enumerate(zip(sources, kept, strict=True))]
    for load in loads:
        load.start()
    q_ref, k_ref, v_ref, taps_ref, filter_ref, bias_ref, gain_ref = kept
    rows, channels = k_ref.shape
    groups = sent_ref.shape[0] // MESSAGE
    each = channels // groups
    for load in (loads[1], loads[2], loads[3]):
        load.wait()
    key = inside(k_ref, taps_ref, 1, padded)
    value = inside(v_ref, taps_ref, 2, padded)
    signal = (key * value).T.reshape(groups, each, rows)
    down = lax.broadcasted_iota(jnp.int32, (rows, rows), 0)
    across = lax.broadcasted_iota(jnp.int32, (rows, rows), 1)
    backwards = (down + across == rows - 1).astype(BF16)
    loads[4].wait()
    taps = jnp.dot(backwards, filter_ref[...].astype(BF16), preferred_element_type=F32)
    taps = taps.T.reshape(groups, each, rows)
    for load in (loads[0], loads[5], loads[6]):
        load.wait()
    start = q_ref[0:16, :].astype(F32)[0:2]
    first = taps_ref[0, 0:1, :] * start
    second = taps_ref[0, 1:2, :] * start[0:1]
    high = bias_ref[...].astype(BF16).astype(F32)
    middle = (bias_ref[...] - high).astype(BF16).astype(F32)
    low = bias_ref[...] - high - middle
    edge = [key[0:2], value[0:2], first[0:1], first[1:2] + second]
    for stream, ref in ((1, k_ref), (2, v_ref), (0, q_ref)):
        edge += into_next(ref, taps_ref, stream)
    edge += [high, middle, low, jnp.zeros((rows - 15, channels), F32)]
    edges[...] = jnp.concatenate(edge, axis=0).T
    edge = edges[pl.ds(0, groups, stride=each), :]
    for c in range(1, each):
        edge = edge + pltpu.roll(edges[pl.ds(c, groups, stride=each), :], EDGE * c, 1)
    blank = jnp.zeros((1, rows), F32)
    messages = []
    for s in range(groups):
        messages += [signal[s], taps[s], edge[s : s + 1], blank]
    sent_ref[...] = jnp.concatenate(messages, axis=0).astype(BF16)
    kept_gain_ref[...] = gain_ref[...]


def conv_kernel(got_ref, out_ref, got, signal, edges, result, phased, *buffers):
    blocks, each, size = out_ref.shape
    step = STEP
    phases = size // step
    steps = blocks * phases
    several = len(buffers) // 2
    windows_refs, toeplitz_refs = buffers[:several], buffers[several:]
    got[...] = got_ref[...].astype(F32)
    lane = lax.broadcasted_iota(jnp.int32, (blocks, size), 1)
    own = lax.broadcasted_iota(jnp.int32, (step, size), 1) < lax.broadcasted_iota(jnp.int32, (step, size), 0) + (size + 1 - step)
    start = lane < 2
    parts = (lane[0:1, :] >= 8) & (lane[0:1, :] < 11)
    edge = got[pl.ds(2 * each, blocks, stride=MESSAGE), :]
    edge = edge + jnp.where(lane % EDGE < 6, pltpu.roll(shift_down(edge, 1), size - 6, 1), 0.0)
    first = edge * pltpu.roll(edge, size - 2, 1)
    for c in range(each):
        at = slice(blocks * c, blocks * c + blocks)
        turned = pltpu.roll(first, size - EDGE * c, 1) if c else first
        signal[at, :] = jnp.where(start, turned, got[pl.ds(c, blocks, stride=MESSAGE), :])
        edges[at, :] = pltpu.roll(edge, (2 * size - EDGE * c - 4) % size, 1)
    for windows_ref in windows_refs:
        windows_ref[:16, :] = jnp.zeros((16, size), F32)

    def rows_of(c):
        return pl.ds(pl.multiple_of(blocks * c, blocks), blocks)

    def steps_of(c, windows_ref):
        now = signal[rows_of(c), :]
        for w in range(phases):
            left = size - step * w - step
            if left:
                turned = pltpu.roll(now, left, 1)
                windows_ref[pl.ds(16 + w, blocks, stride=phases), :] = jnp.where(lane < left, shift_down(turned, 1), turned)
            else:
                windows_ref[pl.ds(16 + w, blocks, stride=phases), :] = now

    def fill(c, toeplitz_ref):
        before = jnp.zeros((step, size), BF16)
        for d in range(blocks):
            spread = jnp.broadcast_to(got[pl.ds(MESSAGE * d + each + c, 1), :], (step, size))
            turned = pltpu.roll(spread, size + 1 - step, 1, stride=1, stride_axis=0).astype(BF16)
            g, back = divmod(d, SPAN)
            at = size * (SPAN - 1 - back)
            toeplitz_ref[step * g : step * g + step, at : at + size] = jnp.where(own, turned, before)
            before = turned

    def later(rows, count):
        return jnp.concatenate([jnp.zeros((count, size), F32), rows[: rows.shape[0] - count]], axis=0) if count else rows

    def finish(c, windows_ref, toeplitz_ref):
        starts = [16 - phases * (SPAN - 1 - u) for u in range(SPAN)]
        windows = jnp.concatenate([windows_ref[a : a + steps, :] for a in starts], axis=1).astype(BF16)
        move = phases * SPAN
        group = size // step
        totals = jnp.zeros((steps, size), F32)
        wide = 2 * size
        for n in range(toeplitz_ref.shape[0] // wide):
            rows = steps - 2 * n * group * move
            product = lax.dot_general(
                windows[:rows],
                toeplitz_ref[wide * n : wide * n + wide, :],
                (((1,), (1,)), ((), ())),
                preferred_element_type=F32,
            )
            for half in range(2):
                count = (2 * n + half) * group * move
                part = product[: steps - count, size * half : size * half + size]
                totals = totals + (jnp.concatenate([jnp.zeros((count, size), F32), part], axis=0) if count else part)
        together = totals
        for i in range(1, group):
            together = together + later(pltpu.roll(totals, size - step * i, 1), move * i)
        phased[...] = together
        out = phased[pl.ds(0, blocks, stride=phases), :]
        for w in range(1, phases):
            out = jnp.where(lane < step * w, out, pltpu.roll(phased[pl.ds(w, blocks, stride=phases), :], step * w, 1))
        edge = edges[rows_of(c), :]
        direct = jnp.sum(jnp.where(parts, edge[0:1, :], 0.0), axis=1, keepdims=True)
        mixed = out + direct * signal[rows_of(c), :]
        result[pl.ds(c, blocks, stride=each), :] = mixed * jnp.where(start, edge, 1.0)

    def channels(i, carry):
        for k in range(several):
            steps_of(several * i + k, windows_refs[k])
            fill(several * i + k, toeplitz_refs[k])
        for k in range(several):
            finish(several * i + k, windows_refs[k], toeplitz_refs[k])
        return carry

    lax.fori_loop(0, each // several, channels, 0)
    out_ref[...] = result[...].reshape(blocks, each, size).astype(BF16)


def mix_kernel(back_ref, q_ref, taps_ref, mixed_ref, squares_ref, padded):
    rows, channels = q_ref.shape
    query = inside(q_ref, taps_ref, 0, padded)
    back = back_ref[...].astype(F32).reshape(channels, rows).T
    row = lax.broadcasted_iota(jnp.int32, (rows, channels), 0)
    mixed = back * jnp.where(row < 2, 1.0, query)
    mixed_ref[...] = mixed
    sums = jnp.sum(mixed * mixed, axis=1, keepdims=True)
    squares_ref[...] = jnp.broadcast_to(sums, (rows, rows)).T[0:1, :]


def norm_kernel(total, squares_ref, mixed_ref, gain_ref, rounded_ref, out_ref):
    rows = mixed_ref.shape[0]
    rounded_ref[...] = mixed_ref[...].astype(BF16)
    squares = jnp.sum(squares_ref[...], axis=0)
    scale = lax.rsqrt(squares / total + EPS)
    scale = jnp.broadcast_to(scale, (rows, rows)).T[:, 0:1]
    out_ref[...] = (mixed_ref[...] * scale * gain_ref[...]).astype(BF16)


def shards(q_proj, k_proj, v_proj, feat_filter, long_filter, skip_bias, norm_gain):
    rows, channels = q_proj.shape
    groups = lax.axis_size("seq")
    columns = lax.axis_size("ch")
    each = channels // groups
    padded = pltpu.VMEM((rows + 8, channels), F32)
    sources = (q_proj, k_proj, v_proj, feat_filter, long_filter, skip_bias.reshape(1, channels), norm_gain.reshape(1, channels))
    sent, kept_gain = pl.pallas_call(
        before_kernel,
        out_shape=(
            jax.ShapeDtypeStruct((groups * MESSAGE, rows), BF16),
            jax.ShapeDtypeStruct((1, channels), F32),
        ),
        in_specs=[HBM] * 7,
        out_specs=(VMEM, VMEM),
        scratch_shapes=[padded, pltpu.VMEM((channels, rows), F32)] + [pltpu.VMEM(a.shape, a.dtype) for a in sources] + [pltpu.SemaphoreType.DMA((7,))],
        compiler_params=PARAMS,
        name="before",
    )(*(pltpu.with_memory_space_constraint(a, pltpu.HBM) for a in sources))
    sent = sent.reshape(groups, MESSAGE // 2, 2, rows)
    got = lax.all_to_all(sent, "seq", split_axis=0, concat_axis=0, tiled=True).reshape(groups * MESSAGE, rows)
    scratch = pltpu.VMEM((groups * each, rows), F32)
    conv = pl.pallas_call(
        conv_kernel,
        out_shape=jax.ShapeDtypeStruct((groups, each, rows), BF16),
        in_specs=[VMEM],
        out_specs=VMEM,
        scratch_shapes=[pltpu.VMEM((groups * MESSAGE, rows), F32)]
        + [scratch] * 3
        + [pltpu.VMEM((groups * rows // STEP, rows), F32)]
        + [pltpu.VMEM((groups * rows // STEP + 16, rows), F32)] * TOGETHER
        + [pltpu.VMEM((STEP * groups // SPAN, SPAN * rows), BF16)] * TOGETHER,
        compiler_params=PARAMS,
        name="conv",
    )(got)
    back = lax.all_to_all(conv, "seq", split_axis=0, concat_axis=0, tiled=True)
    mixed, squares = pl.pallas_call(
        mix_kernel,
        out_shape=(
            jax.ShapeDtypeStruct((rows, channels), F32),
            jax.ShapeDtypeStruct((1, rows), F32),
        ),
        in_specs=[VMEM] * 3,
        out_specs=(VMEM, VMEM),
        scratch_shapes=[padded],
        compiler_params=PARAMS,
        name="mix",
    )(back, q_proj, feat_filter)
    squares = lax.all_gather(squares, "ch")
    rounded, normed = pl.pallas_call(
        lambda *refs: norm_kernel(float(columns * channels), *refs),
        out_shape=(jax.ShapeDtypeStruct((rows, channels), BF16),) * 2,
        in_specs=[VMEM] * 3,
        out_specs=(VMEM, VMEM),
        compiler_params=PARAMS,
        name="norm",
    )(squares, mixed, kept_gain)
    return (rounded, normed)


def solution(mesh):
    return jax.shard_map(
        shards,
        mesh=mesh,
        in_specs=(
            P("seq", "ch"),
            P("seq", "ch"),
            P("seq", "ch"),
            P(None, None, "ch"),
            P("seq", "ch"),
            P("ch"),
            P("ch"),
        ),
        out_specs=(P("seq", "ch"), P("seq", "ch")),
        check_vma=False,
    )
```

time: 85.3 us -> 83.5 us (0.979)
  Pallas kernels: 8.58 us -> 6.75 us
    pallas_call x1, Pallas kernels: 5.13 us -> 3.69 us  [shards(): pl.pallas_call(conv_kernel, out_shape=jax.ShapeDtypeStruct((groups, each,...]
where the time goes in v5:
time: 83.5 us; the launch traced here: 83.3 us
  blocking collectives  75.9 us (91%)
  Pallas kernels  6.75 us (8%)
    all_to_all x1, blocking collectives, shards(): lax.all_to_all(sent, 'seq', split_axis=0, concat_axis=0, tiled=True)  39.6 us
    all_to_all x1, blocking collectives, shards(): back = lax.all_to_all(conv, 'seq', split_axis=0, concat_axis=0, tiled=True)  22.4 us
    all_gather x1, blocking collectives, shards(): squares = lax.all_gather(squares, 'ch')  13.9 us
    pallas_call x1, Pallas kernels, shards(): pl.pallas_call(conv_kernel, out_shape=jax.ShapeDtypeStruct((groups, each,...  3.69 us
    pallas_call x1, Pallas kernels, shards(): pl.pallas_call(before_kernel, out_shape=(jax.ShapeDtypeStruct((groups * M...  1.98 us

profile of v5, /device:TPU:1, one launch (start us, length us, event | category | flops | bytes accessed | tf_op | source)
XLA Modules:
  0.0 83.3 jit_solution(8158801733668705709)
XLA Ops:
  0.6 2.0 %before.1 = (bf16[1152,128]{1,0:T(8,128)(2,1)S(1)}, f32[1,512]{1,0:T(1,128)S(1)}) custom-call(bf16[128,512]{1,0:T(8,128)(2,1)} %q_ref.1, bf16[128,512]{1,0:T(8,128)(2,1)} %refs_1_.1, bf16[128,512]{1,0:T(8,128)(2,1)} %refs_2_.1, f32[3,3,512]{2,1,0:T(4,128)} %taps_ref.1, f32[128,512]{1,0:T(8,128)} %refs_4_.1, f32[1,512]{1,0:T(1,128)} %bitcast.8, f32[1,512]{1,0:T(1,128)} %bitcast.9), custom_call_target="tpu_custom_call" | custom-call | tf_op jit(solution)/shard_map/before/pallas_call | solution.py:204
  2.6 39.6 %all_to_all.10 = bf16[64,9,2,128]{3,2,1,0:T(2,128)(2,1)S(1)} all-to-all(bf16[64,9,2,128]{3,2,1,0:T(2,128)(2,1)S(1)} %bitcast.6), channel_id=1, replica_groups=mesh['seq'=64,'ch'=8] {'seq'}, dimensions={0} | all-to-all | bytes 589824 | tf_op jit(solution)/shard_map/all_to_all | solution.py:217
  42.2 3.7 %conv.1 = bf16[64,8,128]{2,1,0:T(8,128)(2,1)S(1)} custom-call(bf16[1152,128]{1,0:T(8,128)(2,1)S(1)} %bitcast.5), custom_call_target="tpu_custom_call" | custom-call | tf_op jit(solution)/shard_map/conv/pallas_call | solution.py:219
  45.9 0.0 copy-start
  45.9 0.0 copy-start.1
  45.9 22.4 %all_to_all.11.back_ref = bf16[64,8,128]{2,1,0:T(8,128)(2,1)S(1)} all-to-all(bf16[64,8,128]{2,1,0:T(8,128)(2,1)S(1)} %conv.1), channel_id=1, replica_groups=mesh['seq'=64,'ch'=8] {'seq'}, dimensions={0} | all-to-all | bytes 262144 | tf_op jit(solution)/shard_map/all_to_all | solution.py:232
  68.3 0.0 copy-done
  68.3 0.0 copy-done.1
  68.3 0.2 mix.1
  68.5 13.9 %all-gather.1.refs_0_ = f32[8,1,128]{2,1,0:T(1,128)S(1)} all-gather(f32[1,1,128]{2,1,0:T(1,128)S(1)} %bitcast.7), channel_id=2, replica_groups=mesh['seq'=64,'ch'=8] {'ch'}, dimensions={0}, use_global_device_ids=true | all-gather | bytes 4608 | tf_op jit(solution)/shard_map/all_gather | solution.py:245
  82.5 0.8 %norm.1 = (bf16[128,512]{1,0:T(8,128)(2,1)}, bf16[128,512]{1,0:T(8,128)(2,1)}) custom-call(f32[8,1,128]{2,1,0:T(1,128)S(1)} %all-gather.1.refs_0_, f32[128,512]{1,0:T(8,128)S(1)} %get-tuple-element.8.refs_1_, f32[1,512]{1,0:T(1,128)S(1)} %get-tuple-element.9.refs_2_), custom_call_target="tpu_custom_call" | custom-call | tf_op jit(solution)/shard_map/norm/pallas_call | solution.py:246
Async XLA Ops:
  45.9 22.4 %copy-start = (bf16[128,512]{1,0:T(8,128)(2,1)S(1)}, bf16[128,512]{1,0:T(8,128)(2,1)}, u32[]{:S(2)}) copy-start(bf16[128,512]{1,0:T(8,128)(2,1)} %q_ref.1) | copy-start | bytes 393220
  45.9 22.4 %copy-start.1 = (f32[3,3,512]{2,1,0:T(4,128)S(1)}, f32[3,3,512]{2,1,0:T(4,128)}, u32[]{:S(2)}) copy-start(f32[3,3,512]{2,1,0:T(4,128)} %taps_ref.1) | copy-start | bytes 55300

commit v6 on v5

--- a/solution.py
+++ b/solution.py
@@ -44,22 +44,19 @@
     for load in loads:
         load.start()
     q_ref, k_ref, v_ref, taps_ref, filter_ref, bias_ref, gain_ref = kept
+    for load in loads:
+        load.wait()
     rows, channels = k_ref.shape
     groups = sent_ref.shape[0] // MESSAGE
     each = channels // groups
-    for load in (loads[1], loads[2], loads[3]):
-        load.wait()
     key = inside(k_ref, taps_ref, 1, padded)
     value = inside(v_ref, taps_ref, 2, padded)
     signal = (key * value).T.reshape(groups, each, rows)
     down = lax.broadcasted_iota(jnp.int32, (rows, rows), 0)
     across = lax.broadcasted_iota(jnp.int32, (rows, rows), 1)
     backwards = (down + across == rows - 1).astype(BF16)
-    loads[4].wait()
     taps = jnp.dot(backwards, filter_ref[...].astype(BF16), preferred_element_type=F32)
     taps = taps.T.reshape(groups, each, rows)
-    for load in (loads[0], loads[5], loads[6]):
-        load.wait()
     start = q_ref[0:16, :].astype(F32)[0:2]
     first = taps_ref[0, 0:1, :] * start
     second = taps_ref[0, 1:2, :] * start[0:1]
@@ -182,13 +179,13 @@
     mixed = back * jnp.where(row < 2, 1.0, query)
     mixed_ref[...] = mixed
     sums = jnp.sum(mixed * mixed, axis=1, keepdims=True)
-    squares_ref[...] = jnp.broadcast_to(sums, (rows, rows)).T[0:1, :]
+    squares_ref[...] = jnp.broadcast_to(sums, (rows, rows)).T[: squares_ref.shape[0]]
 
 
 def norm_kernel(total, squares_ref, mixed_ref, gain_ref, rounded_ref, out_ref):
     rows = mixed_ref.shape[0]
     rounded_ref[...] = mixed_ref[...].astype(BF16)
-    squares = jnp.sum(squares_ref[...], axis=0)
+    squares = jnp.sum(squares_ref[...], axis=0, keepdims=True)
     scale = lax.rsqrt(squares / total + EPS)
     scale = jnp.broadcast_to(scale, (rows, rows)).T[:, 0:1]
     out_ref[...] = (mixed_ref[...] * scale * gain_ref[...]).astype(BF16)
@@ -234,7 +231,7 @@
         mix_kernel,
         out_shape=(
             jax.ShapeDtypeStruct((rows, channels), F32),
-            jax.ShapeDtypeStruct((1, rows), F32),
+            jax.ShapeDtypeStruct((columns, rows), F32),
         ),
         in_specs=[VMEM] * 3,
         out_specs=(VMEM, VMEM),
@@ -242,7 +239,7 @@
         compiler_params=PARAMS,
         name="mix",
     )(back, q_proj, feat_filter)
-    squares = lax.all_gather(squares, "ch")
+    squares = lax.all_to_all(squares, "ch", split_axis=0, concat_axis=0, tiled=True)
     rounded, normed = pl.pallas_call(
         lambda *refs: norm_kernel(float(columns * channels), *refs),
         out_shape=(jax.ShapeDtypeStruct((rows, channels), BF16),) * 2,

time: 83.5 us -> 81.7 us (0.978)
  blocking collectives: 75.9 us -> 74.3 us
    all_gather x1 -> x0, blocking collectives: 13.9 us -> none  [shards(): squares = lax.all_gather(squares, 'ch')]
    all_to_all x0 -> x1, blocking collectives: none -> 12.3 us  [shards(): lax.all_to_all(squares, 'ch', split_axis=0, concat_axis=0, tiled=True)]
where the time goes in v6:
time: 81.7 us; the launch traced here: 81.5 us
  blocking collectives  74.3 us (91%)
  Pallas kernels  6.57 us (8%)
    all_to_all x1, blocking collectives, shards(): lax.all_to_all(sent, 'seq', split_axis=0, concat_axis=0, tiled=True)  39.6 us
    all_to_all x1, blocking collectives, shards(): back = lax.all_to_all(conv, 'seq', split_axis=0, concat_axis=0, tiled=True)  22.4 us
    all_to_all x1, blocking collectives, shards(): lax.all_to_all(squares, 'ch', split_axis=0, concat_axis=0, tiled=True)  12.3 us
    pallas_call x1, Pallas kernels, shards(): pl.pallas_call(conv_kernel, out_shape=jax.ShapeDtypeStruct((groups, each,...  3.69 us
    pallas_call x1, Pallas kernels, shards(): pl.pallas_call(before_kernel, out_shape=(jax.ShapeDtypeStruct((groups * M...  1.81 us

profile of v6, /device:TPU:1, one launch (start us, length us, event | category | flops | bytes accessed | tf_op | source)
XLA Modules:
  0.0 81.5 jit_solution(5225834443216196235)
XLA Ops:
  0.6 1.8 %before.1 = (bf16[1152,128]{1,0:T(8,128)(2,1)S(1)}, f32[1,512]{1,0:T(1,128)S(1)}) custom-call(bf16[128,512]{1,0:T(8,128)(2,1)} %q_ref.1, bf16[128,512]{1,0:T(8,128)(2,1)} %refs_1_.1, bf16[128,512]{1,0:T(8,128)(2,1)} %refs_2_.1, f32[3,3,512]{2,1,0:T(4,128)} %taps_ref.1, f32[128,512]{1,0:T(8,128)} %refs_4_.1, f32[1,512]{1,0:T(1,128)} %bitcast.12, ...), custom_call_target="tpu_custom_call" | custom-call | tf_op jit(solution)/shard_map/before/pallas_call | solution.py:201
  2.4 39.6 %all_to_all.21 = bf16[64,9,2,128]{3,2,1,0:T(2,128)(2,1)S(1)} all-to-all(bf16[64,9,2,128]{3,2,1,0:T(2,128)(2,1)S(1)} %bitcast.9), channel_id=1, replica_groups=mesh['seq'=64,'ch'=8] {'seq'}, dimensions={0} | all-to-all | bytes 589824 | tf_op jit(solution)/shard_map/all_to_all | solution.py:214
  42.0 3.7 %conv.1 = bf16[64,8,128]{2,1,0:T(8,128)(2,1)S(1)} custom-call(bf16[1152,128]{1,0:T(8,128)(2,1)S(1)} %bitcast.8), custom_call_target="tpu_custom_call" | custom-call | tf_op jit(solution)/shard_map/conv/pallas_call | solution.py:216
  45.7 0.0 copy-start
  45.7 0.0 copy-start.1
  45.7 22.4 %all_to_all.22.back_ref = bf16[64,8,128]{2,1,0:T(8,128)(2,1)S(1)} all-to-all(bf16[64,8,128]{2,1,0:T(8,128)(2,1)S(1)} %conv.1), channel_id=1, replica_groups=mesh['seq'=64,'ch'=8] {'seq'}, dimensions={0} | all-to-all | bytes 262144 | tf_op jit(solution)/shard_map/all_to_all | solution.py:229
  68.1 0.0 copy-done
  68.1 0.0 copy-done.1
  68.1 0.2 mix.1
  68.4 12.3 %all_to_all.23 = f32[8,1,128]{2,1,0:T(1,128)S(1)} all-to-all(f32[8,1,128]{2,1,0:T(1,128)S(1)} %bitcast.11), channel_id=1, replica_groups=mesh['seq'=64,'ch'=8] {'ch'}, dimensions={0} | all-to-all | bytes 8192 | tf_op jit(solution)/shard_map/all_to_all | solution.py:242
  80.7 0.8 %norm.1 = (bf16[128,512]{1,0:T(8,128)(2,1)}, bf16[128,512]{1,0:T(8,128)(2,1)}) custom-call(f32[8,128]{1,0:T(8,128)S(1)} %bitcast.10, f32[128,512]{1,0:T(8,128)S(1)} %get-tuple-element.8.refs_1_, f32[1,512]{1,0:T(1,128)S(1)} %get-tuple-element.9.refs_2_), custom_call_target="tpu_custom_call" | custom-call | tf_op jit(solution)/shard_map/norm/pallas_call | solution.py:243
Async XLA Ops:
  45.7 22.4 %copy-start = (bf16[128,512]{1,0:T(8,128)(2,1)S(1)}, bf16[128,512]{1,0:T(8,128)(2,1)}, u32[]{:S(2)}) copy-start(bf16[128,512]{1,0:T(8,128)(2,1)} %q_ref.1) | copy-start | bytes 393220
  45.7 22.4 %copy-start.1 = (f32[3,3,512]{2,1,0:T(4,128)S(1)}, f32[3,3,512]{2,1,0:T(4,128)}, u32[]{:S(2)}) copy-start(f32[3,3,512]{2,1,0:T(4,128)} %taps_ref.1) | copy-start | bytes 55300

commit v7 on v6

--- a/solution.py
+++ b/solution.py
@@ -12,10 +12,10 @@
 HBM = pl.BlockSpec(memory_space=pltpu.HBM)
 PARAMS = pltpu.CompilerParams(vmem_limit_bytes=16 * 2**20)
 STEP = 32
-SPAN = 4
+SPAN = 2
 MESSAGE = 18
 EDGE = 16
-TOGETHER = 4
+TOGETHER = 8
 
 
 def shift_down(block, count):
@@ -102,6 +102,8 @@
     for windows_ref in windows_refs:
         windows_ref[:16, :] = jnp.zeros((16, size), F32)
 
+    phased[: phased.shape[0] - steps, :] = jnp.zeros((phased.shape[0] - steps, size), F32)
+
     def rows_of(c):
         return pl.ds(pl.multiple_of(blocks * c, blocks), blocks)
 
@@ -124,9 +126,6 @@
             at = size * (SPAN - 1 - back)
             toeplitz_ref[step * g : step * g + step, at : at + size] = jnp.where(own, turned, before)
             before = turned
-
-    def later(rows, count):
-        return jnp.concatenate([jnp.zeros((count, size), F32), rows[: rows.shape[0] - count]], axis=0) if count else rows
 
     def finish(c, windows_ref, toeplitz_ref):
         starts = [16 - phases * (SPAN - 1 - u) for u in range(SPAN)]
@@ -147,13 +146,15 @@
                 count = (2 * n + half) * group * move
                 part = product[: steps - count, size * half : size * half + size]
                 totals = totals + (jnp.concatenate([jnp.zeros((count, size), F32), part], axis=0) if count else part)
-        together = totals
-        for i in range(1, group):
-            together = together + later(pltpu.roll(totals, size - step * i, 1), move * i)
-        phased[...] = together
-        out = phased[pl.ds(0, blocks, stride=phases), :]
-        for w in range(1, phases):
-            out = jnp.where(lane < step * w, out, pltpu.roll(phased[pl.ds(w, blocks, stride=phases), :], step * w, 1))
+        ahead = move * (group - 1)
+        phased[ahead:, :] = totals
+        out = None
+        for r in range(phases):
+            mine = None
+            for i in range(group):
+                source = phased[pl.ds(ahead - move * i + (i + r) % phases, blocks, stride=phases), :]
+                mine = jnp.where(lane < step * i, mine, source) if i else source
+            out = out + pltpu.roll(mine, step * r, 1) if r else mine
         edge = edges[rows_of(c), :]
         direct = jnp.sum(jnp.where(parts, edge[0:1, :], 0.0), axis=1, keepdims=True)
         mixed = out + direct * signal[rows_of(c), :]
@@ -220,7 +221,7 @@
         out_specs=VMEM,
         scratch_shapes=[pltpu.VMEM((groups * MESSAGE, rows), F32)]
         + [scratch] * 3
-        + [pltpu.VMEM((groups * rows // STEP, rows), F32)]
+        + [pltpu.VMEM((groups * rows // STEP + (rows // STEP - 1) * SPAN * rows // STEP, rows), F32)]
         + [pltpu.VMEM((groups * rows // STEP + 16, rows), F32)] * TOGETHER
         + [pltpu.VMEM((STEP * groups // SPAN, SPAN * rows), BF16)] * TOGETHER,
         compiler_params=PARAMS,

time: 81.7 us -> 80.3 us (0.983)
  Pallas kernels: 6.57 us -> 5.13 us
    pallas_call x1, Pallas kernels: 3.69 us -> 2.25 us  [shards(): pl.pallas_call(conv_kernel, out_shape=jax.ShapeDtypeStruct((groups, each,...]
where the time goes in v7:
time: 80.3 us; the launch traced here: 80.1 us
  blocking collectives  74.3 us (93%)
  Pallas kernels  5.13 us (6%)
    all_to_all x1, blocking collectives, shards(): lax.all_to_all(sent, 'seq', split_axis=0, concat_axis=0, tiled=True)  39.6 us
    all_to_all x1, blocking collectives, shards(): back = lax.all_to_all(conv, 'seq', split_axis=0, concat_axis=0, tiled=True)  22.4 us
    all_to_all x1, blocking collectives, shards(): lax.all_to_all(squares, 'ch', split_axis=0, concat_axis=0, tiled=True)  12.3 us
    pallas_call x1, Pallas kernels, shards(): pl.pallas_call(conv_kernel, out_shape=jax.ShapeDtypeStruct((groups, each,...  2.25 us
    pallas_call x1, Pallas kernels, shards(): pl.pallas_call(before_kernel, out_shape=(jax.ShapeDtypeStruct((groups * M...  1.81 us

profile of v7, /device:TPU:1, one launch (start us, length us, event | category | flops | bytes accessed | tf_op | source)
XLA Modules:
  0.0 80.1 jit_solution(13990441533969137122)
XLA Ops:
  0.6 1.8 %before.1 = (bf16[1152,128]{1,0:T(8,128)(2,1)S(1)}, f32[1,512]{1,0:T(1,128)S(1)}) custom-call(bf16[128,512]{1,0:T(8,128)(2,1)} %q_ref.1, bf16[128,512]{1,0:T(8,128)(2,1)} %refs_1_.1, bf16[128,512]{1,0:T(8,128)(2,1)} %refs_2_.1, f32[3,3,512]{2,1,0:T(4,128)} %taps_ref.1, f32[128,512]{1,0:T(8,128)} %refs_4_.1, f32[1,512]{1,0:T(1,128)} %bitcast.12, ...), custom_call_target="tpu_custom_call" | custom-call | tf_op jit(solution)/shard_map/before/pallas_call | solution.py:202
  2.4 39.6 %all_to_all.21 = bf16[64,9,2,128]{3,2,1,0:T(2,128)(2,1)S(1)} all-to-all(bf16[64,9,2,128]{3,2,1,0:T(2,128)(2,1)S(1)} %bitcast.9), channel_id=1, replica_groups=mesh['seq'=64,'ch'=8] {'seq'}, dimensions={0} | all-to-all | bytes 589824 | tf_op jit(solution)/shard_map/all_to_all | solution.py:215
  42.0 2.2 %conv.1 = bf16[64,8,128]{2,1,0:T(8,128)(2,1)S(1)} custom-call(bf16[1152,128]{1,0:T(8,128)(2,1)S(1)} %bitcast.8), custom_call_target="tpu_custom_call" | custom-call | tf_op jit(solution)/shard_map/conv/pallas_call | solution.py:217
  44.3 0.0 copy-start
  44.3 0.0 copy-start.1
  44.3 22.4 %all_to_all.22.back_ref = bf16[64,8,128]{2,1,0:T(8,128)(2,1)S(1)} all-to-all(bf16[64,8,128]{2,1,0:T(8,128)(2,1)S(1)} %conv.1), channel_id=1, replica_groups=mesh['seq'=64,'ch'=8] {'seq'}, dimensions={0} | all-to-all | bytes 262144 | tf_op jit(solution)/shard_map/all_to_all | solution.py:230
  66.7 0.0 copy-done
  66.7 0.0 copy-done.1
  66.7 0.2 mix.1
  66.9 12.3 %all_to_all.23 = f32[8,1,128]{2,1,0:T(1,128)S(1)} all-to-all(f32[8,1,128]{2,1,0:T(1,128)S(1)} %bitcast.11), channel_id=1, replica_groups=mesh['seq'=64,'ch'=8] {'ch'}, dimensions={0} | all-to-all | bytes 8192 | tf_op jit(solution)/shard_map/all_to_all | solution.py:243
  79.2 0.8 %norm.1 = (bf16[128,512]{1,0:T(8,128)(2,1)}, bf16[128,512]{1,0:T(8,128)(2,1)}) custom-call(f32[8,128]{1,0:T(8,128)S(1)} %bitcast.10, f32[128,512]{1,0:T(8,128)S(1)} %get-tuple-element.8.refs_1_, f32[1,512]{1,0:T(1,128)S(1)} %get-tuple-element.9.refs_2_), custom_call_target="tpu_custom_call" | custom-call | tf_op jit(solution)/shard_map/norm/pallas_call | solution.py:244
Async XLA Ops:
  44.3 22.4 %copy-start = (bf16[128,512]{1,0:T(8,128)(2,1)S(1)}, bf16[128,512]{1,0:T(8,128)(2,1)}, u32[]{:S(2)}) copy-start(bf16[128,512]{1,0:T(8,128)(2,1)} %q_ref.1) | copy-start | bytes 393220
  44.3 22.4 %copy-start.1 = (f32[3,3,512]{2,1,0:T(4,128)S(1)}, f32[3,3,512]{2,1,0:T(4,128)}, u32[]{:S(2)}) copy-start(f32[3,3,512]{2,1,0:T(4,128)} %taps_ref.1) | copy-start | bytes 55300

commit v8 on v7

--- a/solution.py
+++ b/solution.py
@@ -71,10 +71,10 @@
     edge = edges[pl.ds(0, groups, stride=each), :]
     for c in range(1, each):
         edge = edge + pltpu.roll(edges[pl.ds(c, groups, stride=each), :], EDGE * c, 1)
-    blank = jnp.zeros((1, rows), F32)
+    rest = edge - edge.astype(BF16).astype(F32)
     messages = []
     for s in range(groups):
-        messages += [signal[s], taps[s], edge[s : s + 1], blank]
+        messages += [signal[s], taps[s], edge[s : s + 1], rest[s : s + 1]]
     sent_ref[...] = jnp.concatenate(messages, axis=0).astype(BF16)
     kept_gain_ref[...] = gain_ref[...]
 
@@ -91,7 +91,7 @@
     own = lax.broadcasted_iota(jnp.int32, (step, size), 1) < lax.broadcasted_iota(jnp.int32, (step, size), 0) + (size + 1 - step)
     start = lane < 2
     parts = (lane[0:1, :] >= 8) & (lane[0:1, :] < 11)
-    edge = got[pl.ds(2 * each, blocks, stride=MESSAGE), :]
+    edge = got[pl.ds(2 * each, blocks, stride=MESSAGE), :] + got[pl.ds(2 * each + 1, blocks, stride=MESSAGE), :]
     edge = edge + jnp.where(lane % EDGE < 6, pltpu.roll(shift_down(edge, 1), size - 6, 1), 0.0)
     first = edge * pltpu.roll(edge, size - 2, 1)
     for c in range(each):

time: 80.3 us -> 80.3 us (level)
  no operation moved by 1% of the time
where the time goes in v8:
time: 80.3 us; the launch traced here: 80.1 us
  blocking collectives  74.3 us (93%)
  Pallas kernels  5.14 us (6%)
    all_to_all x1, blocking collectives, shards(): lax.all_to_all(sent, 'seq', split_axis=0, concat_axis=0, tiled=True)  39.6 us
    all_to_all x1, blocking collectives, shards(): back = lax.all_to_all(conv, 'seq', split_axis=0, concat_axis=0, tiled=True)  22.4 us
    all_to_all x1, blocking collectives, shards(): lax.all_to_all(squares, 'ch', split_axis=0, concat_axis=0, tiled=True)  12.3 us
    pallas_call x1, Pallas kernels, shards(): pl.pallas_call(conv_kernel, out_shape=jax.ShapeDtypeStruct((groups, each,...  2.23 us
    pallas_call x1, Pallas kernels, shards(): pl.pallas_call(before_kernel, out_shape=(jax.ShapeDtypeStruct((groups * M...  1.83 us

profile of v8, /device:TPU:1, one launch (start us, length us, event | category | flops | bytes accessed | tf_op | source)
XLA Modules:
  0.0 80.1 jit_solution(7739932620872589659)
XLA Ops:
  0.6 1.8 %before.1 = (bf16[1152,128]{1,0:T(8,128)(2,1)S(1)}, f32[1,512]{1,0:T(1,128)S(1)}) custom-call(bf16[128,512]{1,0:T(8,128)(2,1)} %q_ref.1, bf16[128,512]{1,0:T(8,128)(2,1)} %refs_1_.1, bf16[128,512]{1,0:T(8,128)(2,1)} %refs_2_.1, f32[3,3,512]{2,1,0:T(4,128)} %taps_ref.1, f32[128,512]{1,0:T(8,128)} %refs_4_.1, f32[1,512]{1,0:T(1,128)} %bitcast.12, ...), custom_call_target="tpu_custom_call" | custom-call | tf_op jit(solution)/shard_map/before/pallas_call | solution.py:202
  2.5 39.6 %all_to_all.21 = bf16[64,9,2,128]{3,2,1,0:T(2,128)(2,1)S(1)} all-to-all(bf16[64,9,2,128]{3,2,1,0:T(2,128)(2,1)S(1)} %bitcast.9), channel_id=1, replica_groups=mesh['seq'=64,'ch'=8] {'seq'}, dimensions={0} | all-to-all | bytes 589824 | tf_op jit(solution)/shard_map/all_to_all | solution.py:215
  42.0 2.2 %conv.1 = bf16[64,8,128]{2,1,0:T(8,128)(2,1)S(1)} custom-call(bf16[1152,128]{1,0:T(8,128)(2,1)S(1)} %bitcast.8), custom_call_target="tpu_custom_call" | custom-call | tf_op jit(solution)/shard_map/conv/pallas_call | solution.py:217
  44.3 0.0 copy-start
  44.3 0.0 copy-start.1
  44.3 22.4 %all_to_all.22.back_ref = bf16[64,8,128]{2,1,0:T(8,128)(2,1)S(1)} all-to-all(bf16[64,8,128]{2,1,0:T(8,128)(2,1)S(1)} %conv.1), channel_id=1, replica_groups=mesh['seq'=64,'ch'=8] {'seq'}, dimensions={0} | all-to-all | bytes 262144 | tf_op jit(solution)/shard_map/all_to_all | solution.py:230
  66.7 0.0 copy-done
  66.7 0.0 copy-done.1
  66.7 0.2 mix.1
  66.9 12.3 %all_to_all.23 = f32[8,1,128]{2,1,0:T(1,128)S(1)} all-to-all(f32[8,1,128]{2,1,0:T(1,128)S(1)} %bitcast.11), channel_id=1, replica_groups=mesh['seq'=64,'ch'=8] {'ch'}, dimensions={0} | all-to-all | bytes 8192 | tf_op jit(solution)/shard_map/all_to_all | solution.py:243
  79.3 0.8 %norm.1 = (bf16[128,512]{1,0:T(8,128)(2,1)}, bf16[128,512]{1,0:T(8,128)(2,1)}) custom-call(f32[8,128]{1,0:T(8,128)S(1)} %bitcast.10, f32[128,512]{1,0:T(8,128)S(1)} %get-tuple-element.8.refs_1_, f32[1,512]{1,0:T(1,128)S(1)} %get-tuple-element.9.refs_2_), custom_call_target="tpu_custom_call" | custom-call | tf_op jit(solution)/shard_map/norm/pallas_call | solution.py:244
Async XLA Ops:
  44.3 22.4 %copy-start = (bf16[128,512]{1,0:T(8,128)(2,1)S(1)}, bf16[128,512]{1,0:T(8,128)(2,1)}, u32[]{:S(2)}) copy-start(bf16[128,512]{1,0:T(8,128)(2,1)} %q_ref.1) | copy-start | bytes 393220
  44.3 22.4 %copy-start.1 = (f32[3,3,512]{2,1,0:T(4,128)S(1)}, f32[3,3,512]{2,1,0:T(4,128)}, u32[]{:S(2)}) copy-start(f32[3,3,512]{2,1,0:T(4,128)} %taps_ref.1) | copy-start | bytes 55300

commit v9 on v8

--- a/solution.py
+++ b/solution.py
@@ -40,12 +40,15 @@
 
 def before_kernel(*refs):
     sources, (sent_ref, kept_gain_ref, padded, edges, *kept, sems) = refs[:7], refs[7:]
-    loads = [pltpu.make_async_copy(a, b, sems.at[i]) for i, (a, b) in enumerate(zip(sources, kept, strict=True))]
+    pairs = list(zip(sources[1:], kept[1:], strict=True))
+    for at in (pl.ds(0, 16), pl.ds(kept[0].shape[0] - 16, 16)):
+        pairs.append((sources[0].at[at], kept[0].at[at]))
+    loads = [pltpu.make_async_copy(a, b, sems.at[i]) for i, (a, b) in enumerate(pairs)]
     for load in loads:
         load.start()
     q_ref, k_ref, v_ref, taps_ref, filter_ref, bias_ref, gain_ref = kept
-    for load in loads:
-        load.wait()
+    for i in (0, 1, 2, 4, 5, 6, 7):
+        loads[i].wait()
     rows, channels = k_ref.shape
     groups = sent_ref.shape[0] // MESSAGE
     each = channels // groups
@@ -55,6 +58,7 @@
     down = lax.broadcasted_iota(jnp.int32, (rows, rows), 0)
     across = lax.broadcasted_iota(jnp.int32, (rows, rows), 1)
     backwards = (down + across == rows - 1).astype(BF16)
+    loads[3].wait()
     taps = jnp.dot(backwards, filter_ref[...].astype(BF16), preferred_element_type=F32)
     taps = taps.T.reshape(groups, each, rows)
     start = q_ref[0:16, :].astype(F32)[0:2]
@@ -207,7 +211,7 @@
         ),
         in_specs=[HBM] * 7,
         out_specs=(VMEM, VMEM),
-        scratch_shapes=[padded, pltpu.VMEM((channels, rows), F32)] + [pltpu.VMEM(a.shape, a.dtype) for a in sources] + [pltpu.SemaphoreType.DMA((7,))],
+        scratch_shapes=[padded, pltpu.VMEM((channels, rows), F32)] + [pltpu.VMEM(a.shape, a.dtype) for a in sources] + [pltpu.SemaphoreType.DMA((8,))],
         compiler_params=PARAMS,
         name="before",
     )(*(pltpu.with_memory_space_constraint(a, pltpu.HBM) for a in sources))

time: 80.3 us -> 80.3 us (level)
  no operation moved by 1% of the time
where the time goes in v9:
time: 80.3 us; the launch traced here: 80 us
  blocking collectives  74.3 us (93%)
  Pallas kernels  5.06 us (6%)
    all_to_all x1, blocking collectives, shards(): lax.all_to_all(sent, 'seq', split_axis=0, concat_axis=0, tiled=True)  39.6 us
    all_to_all x1, blocking collectives, shards(): back = lax.all_to_all(conv, 'seq', split_axis=0, concat_axis=0, tiled=True)  22.4 us
    all_to_all x1, blocking collectives, shards(): lax.all_to_all(squares, 'ch', split_axis=0, concat_axis=0, tiled=True)  12.3 us
    pallas_call x1, Pallas kernels, shards(): pl.pallas_call(conv_kernel, out_shape=jax.ShapeDtypeStruct((groups, each,...  2.23 us
    pallas_call x1, Pallas kernels, shards(): pl.pallas_call(before_kernel, out_shape=(jax.ShapeDtypeStruct((groups * M...  1.75 us

profile of v9, /device:TPU:1, one launch (start us, length us, event | category | flops | bytes accessed | tf_op | source)
XLA Modules:
  0.0 80.0 jit_solution(16476669257003333960)
XLA Ops:
  0.6 1.8 %before.1 = (bf16[1152,128]{1,0:T(8,128)(2,1)S(1)}, f32[1,512]{1,0:T(1,128)S(1)}) custom-call(bf16[128,512]{1,0:T(8,128)(2,1)} %q_ref.1, bf16[128,512]{1,0:T(8,128)(2,1)} %refs_1_.1, bf16[128,512]{1,0:T(8,128)(2,1)} %refs_2_.1, f32[3,3,512]{2,1,0:T(4,128)} %taps_ref.1, f32[128,512]{1,0:T(8,128)} %refs_4_.1, f32[1,512]{1,0:T(1,128)} %bitcast.12, ...), custom_call_target="tpu_custom_call" | custom-call | tf_op jit(solution)/shard_map/before/pallas_call | solution.py:206
  2.4 39.6 %all_to_all.21 = bf16[64,9,2,128]{3,2,1,0:T(2,128)(2,1)S(1)} all-to-all(bf16[64,9,2,128]{3,2,1,0:T(2,128)(2,1)S(1)} %bitcast.9), channel_id=1, replica_groups=mesh['seq'=64,'ch'=8] {'seq'}, dimensions={0} | all-to-all | bytes 589824 | tf_op jit(solution)/shard_map/all_to_all | solution.py:219
  41.9 2.2 %conv.1 = bf16[64,8,128]{2,1,0:T(8,128)(2,1)S(1)} custom-call(bf16[1152,128]{1,0:T(8,128)(2,1)S(1)} %bitcast.8), custom_call_target="tpu_custom_call" | custom-call | tf_op jit(solution)/shard_map/conv/pallas_call | solution.py:221
  44.2 0.0 copy-start
  44.2 0.0 copy-start.1
  44.2 22.4 %all_to_all.22.back_ref = bf16[64,8,128]{2,1,0:T(8,128)(2,1)S(1)} all-to-all(bf16[64,8,128]{2,1,0:T(8,128)(2,1)S(1)} %conv.1), channel_id=1, replica_groups=mesh['seq'=64,'ch'=8] {'seq'}, dimensions={0} | all-to-all | bytes 262144 | tf_op jit(solution)/shard_map/all_to_all | solution.py:234
  66.6 0.0 copy-done
  66.6 0.0 copy-done.1
  66.6 0.2 mix.1
  66.9 12.3 %all_to_all.23 = f32[8,1,128]{2,1,0:T(1,128)S(1)} all-to-all(f32[8,1,128]{2,1,0:T(1,128)S(1)} %bitcast.11), channel_id=1, replica_groups=mesh['seq'=64,'ch'=8] {'ch'}, dimensions={0} | all-to-all | bytes 8192 | tf_op jit(solution)/shard_map/all_to_all | solution.py:247
  79.2 0.8 %norm.1 = (bf16[128,512]{1,0:T(8,128)(2,1)}, bf16[128,512]{1,0:T(8,128)(2,1)}) custom-call(f32[8,128]{1,0:T(8,128)S(1)} %bitcast.10, f32[128,512]{1,0:T(8,128)S(1)} %get-tuple-element.8.refs_1_, f32[1,512]{1,0:T(1,128)S(1)} %get-tuple-element.9.refs_2_), custom_call_target="tpu_custom_call" | custom-call | tf_op jit(solution)/shard_map/norm/pallas_call | solution.py:248
Async XLA Ops:
  44.2 22.4 %copy-start = (bf16[128,512]{1,0:T(8,128)(2,1)S(1)}, bf16[128,512]{1,0:T(8,128)(2,1)}, u32[]{:S(2)}) copy-start(bf16[128,512]{1,0:T(8,128)(2,1)} %q_ref.1) | copy-start | bytes 393220
  44.2 22.4 %copy-start.1 = (f32[3,3,512]{2,1,0:T(4,128)S(1)}, f32[3,3,512]{2,1,0:T(4,128)}, u32[]{:S(2)}) copy-start(f32[3,3,512]{2,1,0:T(4,128)} %taps_ref.1) | copy-start | bytes 55300

commit v10 on v8

--- a/solution.py
+++ b/solution.py
@@ -15,7 +15,7 @@
 SPAN = 2
 MESSAGE = 18
 EDGE = 16
-TOGETHER = 8
+TOGETHER = 4
 
 
 def shift_down(block, count):

time: 80.3 us -> 80.6 us (level)
  no operation moved by 1% of the time
where the time goes in v10:
time: 80.6 us; the launch traced here: 80.4 us
  blocking collectives  74.3 us (92%)
  Pallas kernels  5.42 us (7%)
    all_to_all x1, blocking collectives, shards(): lax.all_to_all(sent, 'seq', split_axis=0, concat_axis=0, tiled=True)  39.6 us
    all_to_all x1, blocking collectives, shards(): back = lax.all_to_all(conv, 'seq', split_axis=0, concat_axis=0, tiled=True)  22.4 us
    all_to_all x1, blocking collectives, shards(): lax.all_to_all(squares, 'ch', split_axis=0, concat_axis=0, tiled=True)  12.3 us
    pallas_call x1, Pallas kernels, shards(): pl.pallas_call(conv_kernel, out_shape=jax.ShapeDtypeStruct((groups, each,...  2.51 us
    pallas_call x1, Pallas kernels, shards(): pl.pallas_call(before_kernel, out_shape=(jax.ShapeDtypeStruct((groups * M...  1.83 us

profile of v10, /device:TPU:1, one launch (start us, length us, event | category | flops | bytes accessed | tf_op | source)
XLA Modules:
  0.0 80.4 jit_solution(3094721118008577971)
XLA Ops:
  0.6 1.8 %before.1 = (bf16[1152,128]{1,0:T(8,128)(2,1)S(1)}, f32[1,512]{1,0:T(1,128)S(1)}) custom-call(bf16[128,512]{1,0:T(8,128)(2,1)} %q_ref.1, bf16[128,512]{1,0:T(8,128)(2,1)} %refs_1_.1, bf16[128,512]{1,0:T(8,128)(2,1)} %refs_2_.1, f32[3,3,512]{2,1,0:T(4,128)} %taps_ref.1, f32[128,512]{1,0:T(8,128)} %refs_4_.1, f32[1,512]{1,0:T(1,128)} %bitcast.12, ...), custom_call_target="tpu_custom_call" | custom-call | tf_op jit(solution)/shard_map/before/pallas_call | solution.py:202
  2.5 39.6 %all_to_all.21 = bf16[64,9,2,128]{3,2,1,0:T(2,128)(2,1)S(1)} all-to-all(bf16[64,9,2,128]{3,2,1,0:T(2,128)(2,1)S(1)} %bitcast.9), channel_id=1, replica_groups=mesh['seq'=64,'ch'=8] {'seq'}, dimensions={0} | all-to-all | bytes 589824 | tf_op jit(solution)/shard_map/all_to_all | solution.py:215
  42.0 2.5 %conv.1 = bf16[64,8,128]{2,1,0:T(8,128)(2,1)S(1)} custom-call(bf16[1152,128]{1,0:T(8,128)(2,1)S(1)} %bitcast.8), custom_call_target="tpu_custom_call" | custom-call | tf_op jit(solution)/shard_map/conv/pallas_call | solution.py:217
  44.5 0.0 copy-start
  44.6 0.0 copy-start.1
  44.6 22.4 %all_to_all.22.back_ref = bf16[64,8,128]{2,1,0:T(8,128)(2,1)S(1)} all-to-all(bf16[64,8,128]{2,1,0:T(8,128)(2,1)S(1)} %conv.1), channel_id=1, replica_groups=mesh['seq'=64,'ch'=8] {'seq'}, dimensions={0} | all-to-all | bytes 262144 | tf_op jit(solution)/shard_map/all_to_all | solution.py:230
  67.0 0.0 copy-done
  67.0 0.0 copy-done.1
  67.0 0.2 mix.1
  67.2 12.3 %all_to_all.23 = f32[8,1,128]{2,1,0:T(1,128)S(1)} all-to-all(f32[8,1,128]{2,1,0:T(1,128)S(1)} %bitcast.11), channel_id=1, replica_groups=mesh['seq'=64,'ch'=8] {'ch'}, dimensions={0} | all-to-all | bytes 8192 | tf_op jit(solution)/shard_map/all_to_all | solution.py:243
  79.5 0.8 %norm.1 = (bf16[128,512]{1,0:T(8,128)(2,1)}, bf16[128,512]{1,0:T(8,128)(2,1)}) custom-call(f32[8,128]{1,0:T(8,128)S(1)} %bitcast.10, f32[128,512]{1,0:T(8,128)S(1)} %get-tuple-element.8.refs_1_, f32[1,512]{1,0:T(1,128)S(1)} %get-tuple-element.9.refs_2_), custom_call_target="tpu_custom_call" | custom-call | tf_op jit(solution)/shard_map/norm/pallas_call | solution.py:244
Async XLA Ops:
  44.5 22.4 %copy-start = (bf16[128,512]{1,0:T(8,128)(2,1)S(1)}, bf16[128,512]{1,0:T(8,128)(2,1)}, u32[]{:S(2)}) copy-start(bf16[128,512]{1,0:T(8,128)(2,1)} %q_ref.1) | copy-start | bytes 393220
  44.6 22.4 %copy-start.1 = (f32[3,3,512]{2,1,0:T(4,128)S(1)}, f32[3,3,512]{2,1,0:T(4,128)}, u32[]{:S(2)}) copy-start(f32[3,3,512]{2,1,0:T(4,128)} %taps_ref.1) | copy-start | bytes 55300
